TPU v7x, 32 devices: a whole 2x2x4 slice. The times are simulated.
32 devices in a mesh: groups: 2 (over y), tm: 4 (over z), space: 2 (over x), clip: 2 (over core).
Axes of the slice: x: 2, y: 2, z: 4, core: 2. Of those that a mesh axis runs over, the one named last changes fastest.
Arguments:
- features: bfloat16 [4, 16, 8, 16, 256], P(('groups', 'clip'), 'tm', 'space'), parts along dimension 0, may hold values from -6 to 6
- frame_counts: int32 [4], P(('groups', 'clip')), parts along dimension 0, may hold values from 1 to 16, as said below
- routes: int32 [4, 512, 1], P(('groups', 'clip'), ('tm', 'space')), parts along dimension 0, may hold values from 0 to 7; in each aligned block of 64 rows (0 to 63, 64 to 127, ..., all dimensions but the last counted through in order) at most 9 rows name the same one
- norm_gains: float32 [3, 256], replicated, may hold values from 0.5 to 1.5
- conv_weights: bfloat16 [2, 256, 27, 256], P(None, 'tm'), may hold values from -0.078125 to 0.078125
- conv_biases: float32 [2, 256], replicated, may hold values from -3 to 3
- latent_weight: bfloat16 [256, 16], replicated, may hold values from -0.375 to 0.375
- embed_weight: bfloat16 [64, 3072], replicated, may hold values from -0.75 to 0.75
- embed_bias: float32 [3072], replicated, may hold values from -3 to 3
Outputs:
- packed: bfloat16 [4, 576, 3072], P(('groups', 'clip'), ('tm', 'space')), parts along dimension 0
There are 2 independent parts, one for each index of `groups`. A program takes and returns all parts, laid end to end along the dimension named above; an argument that names none is the same for every part. Nothing has to cross between parts.
Inputs may be any that keep to these rules, and one draw needn't show every extreme that they name: `routes`: in each clip, the 64 patches of one span and tile name any one owner at most 9 times. `frame_counts`: one clip of each part has all 16 frames valid.
All inputs are finite; a program needn't handle non-finite values.
Results may differ from a plain program's by a relative error of at most 0.0054.
Values may be sent and summed in bfloat16 or wider, within the bound.
A program may use at most 64 MiB of HBM per device.

v0:
```python
import functools

import jax
import jax.numpy as jnp
from jax import lax
from jax.experimental import pallas as pl
from jax.experimental.pallas import tpu as pltpu
from jax.sharding import PartitionSpec as P

MESH = pl.DeviceIdType.MESH
LANES = 128
SUBLANES = 16
CUTS = 4


def norm_silu(values, gain):
    scale = lax.rsqrt(jnp.mean(values * values, axis=-1, keepdims=True) + 1e-06)
    scaled = values * scale * gain
    return scaled / (1.0 + jnp.exp(-scaled))


def encoder(
    n, ns, most, width_latent,
    feat, weights_any, gains, biases, latent_rows, owner_of, count,
    tokens_out,
    first, second, taps, placing, slab_out, slab_in, tok_out, tok_in,
    raw_sem, block_send, block_recv, up_send, up_recv, down_send, down_recv,
    slab_send, slab_recv, tok_send, tok_recv,
):
    t = lax.axis_index("tm")
    s = lax.axis_index("space")
    me = t * ns + s
    owners = n * ns
    frames, rows, cols, width = feat.shape
    cells = frames * rows * cols
    out = weights_any.shape[2] // 3
    cuts = block_recv.shape[2]
    size = frames // cuts
    pack = max(1, LANES // out)
    part = cells // pack

    barrier = pltpu.get_barrier_semaphore()

    def greet(d, carry):
        o = (me + d) % owners
        pl.semaphore_signal(
            barrier, inc=1, device_id={"tm": o // ns, "space": o % ns}, device_id_type=MESH
        )
        return carry

    lax.fori_loop(1, owners, greet, 0)
    weight_copy = pltpu.make_async_copy(weights_any, taps, raw_sem)
    weight_copy.start()

    for buf in (first, second):
        buf[0:2] = jnp.zeros((2,) + buf.shape[1:], buf.dtype)

        @pl.when(s == 0)
        def _():
            buf[:, 0:1] = jnp.zeros((buf.shape[0], 1) + buf.shape[2:], buf.dtype)

        @pl.when(s == ns - 1)
        def _():
            buf[:, rows + 1 : rows + 2] = jnp.zeros((buf.shape[0], 1) + buf.shape[2:], buf.dtype)

    inputs = feat[...].reshape(cells, width).astype(jnp.float32)

    def keep(buf, active):
        buf[pl.ds(2 + frames * t, frames), 1 : rows + 1] = active.astype(jnp.bfloat16).reshape(
            frames, rows, cols, width
        )

    def block_copy(buf, layer, c, f, way):
        span = buf.at[pl.ds(2 + frames * c + size * f, size), pl.ds(1, rows)]
        return pltpu.make_async_remote_copy(
            src_ref=span, dst_ref=span,
            send_sem=block_send.at[layer, way, c, f], recv_sem=block_recv.at[layer, c, f],
            device_id={"tm": (t + 1 - 2 * way + n) % n}, device_id_type=MESH,
        )

    def up_copy(buf, layer, c, f):
        return pltpu.make_async_remote_copy(
            src_ref=buf.at[pl.ds(2 + frames * c + size * f, size), pl.ds(1, 1)],
            dst_ref=buf.at[pl.ds(2 + frames * c + size * f, size), pl.ds(rows + 1, 1)],
            send_sem=up_send.at[layer, c, f], recv_sem=up_recv.at[layer, c, f],
            device_id={"space": (s + ns - 1) % ns}, device_id_type=MESH,
        )

    def down_copy(buf, layer, c, f):
        return pltpu.make_async_remote_copy(
            src_ref=buf.at[pl.ds(2 + frames * c + size * f, size), pl.ds(rows, 1)],
            dst_ref=buf.at[pl.ds(2 + frames * c + size * f, size), pl.ds(0, 1)],
            send_sem=down_send.at[layer, c, f], recv_sem=down_recv.at[layer, c, f],
            device_id={"space": (s + 1) % ns}, device_id_type=MESH,
        )

    def slab_copy(layer, source, target):
        return pltpu.make_async_remote_copy(
            src_ref=slab_out.at[layer, target], dst_ref=slab_in.at[layer, source],
            send_sem=slab_send.at[layer, target], recv_sem=slab_recv.at[layer, source],
            device_id={"tm": target}, device_id_type=MESH,
        )

    def outward(buf, layer, c, f, act):
        pl.when((c <= t) & (t < n - 1))(lambda: act(block_copy(buf, layer, c, f, 0)))
        pl.when((c >= t) & (t > 0))(lambda: act(block_copy(buf, layer, c, f, 1)))
        pl.when(s > 0)(lambda: act(up_copy(buf, layer, c, f)))
        pl.when(s < ns - 1)(lambda: act(down_copy(buf, layer, c, f)))

    def spread(buf, layer):
        for f in range(cuts):
            outward(buf, layer, t, f, lambda copy: copy.start())

    def spread_sent(buf, layer):
        def sent(c, carry):
            for f in range(cuts):
                outward(buf, layer, c, f, lambda copy: copy.wait_send())

            @pl.when(c != t)
            def _():
                slab_copy(layer, t, c).wait_send()

            return carry

        lax.fori_loop(0, n, sent, 0)

    def handle(buf, layer, c, f):
        block_copy(buf, layer, c, f, 0).wait_recv()
        outward(buf, layer, c, f, lambda copy: copy.start())

    def rims(buf, layer, c):
        for f in range(cuts):
            pl.when(s < ns - 1)(lambda: up_copy(buf, layer, c, f).wait_recv())
            pl.when(s > 0)(lambda: down_copy(buf, layer, c, f).wait_recv())

    column = lax.broadcasted_iota(jnp.int32, (cells, 1), 0) % cols

    def convolve(buf, layer):
        def one(b):
            total = jnp.zeros((cells, 3 * out), jnp.float32)
            for a in range(3):
                for r in range(3):
                    block = buf[pl.ds(frames * b + a, frames), r : r + rows]
                    total = total + lax.dot_general(
                        block.reshape(cells, width), taps[layer, 3 * a + r],
                        (((1,), (1,)), ((), ())), preferred_element_type=jnp.float32,
                    )
            left = jnp.where(column == 0, 0.0, pltpu.roll(total[:, :out], 1, 0))
            right = jnp.where(column == cols - 1, 0.0, pltpu.roll(total[:, 2 * out :], cells - 1, 0))
            summed = (left + total[:, out : 2 * out] + right).astype(jnp.bfloat16)
            packed = jnp.concatenate(
                [summed[j * part : (j + 1) * part] for j in range(pack)], axis=1
            )

            @pl.when(b == t)
            def _():
                slab_in[layer, pl.ds(t, 1)] = packed[None]

            @pl.when(b != t)
            def _():
                slab_out[layer, pl.ds(b, 1)] = packed[None]
                slab_copy(layer, t, b).start()

        def ring(d, carry):
            low, high = t - d, t + d
            is_low, is_high = low >= 0, high < n
            for f in range(cuts):
                pl.when(is_low)(lambda: handle(buf, layer, (low + n) % n, f))
                pl.when(is_high)(lambda: handle(buf, layer, high % n, f))
            low, high = low + 1, high - 1
            is_low, is_high = (low >= 0) & (low < t), (high < n) & (high > t)
            pl.when(d == 2)(lambda: rims(buf, layer, t))
            pl.when(is_low)(lambda: rims(buf, layer, (low + n) % n))
            pl.when(is_high)(lambda: rims(buf, layer, high % n))

            def ready(i, carry):
                b = jnp.where(i == 0, high, low + 1)
                pl.when((d > 1) & (b >= 0) & (b < n))(lambda: one((b + n) % n))
                return carry

            lax.fori_loop(0, 2, ready, 0)
            return carry

        lax.fori_loop(1, n + 2, ring, 0)

        def came(k, carry):
            slab_copy(layer, (t + k) % n, (t + k) % n).wait_recv()
            return carry

        lax.fori_loop(1, n, came, 0)
        pieces = [slab_in[layer, q].astype(jnp.float32) for q in range(n)]
        hidden = jnp.concatenate(
            [
                jnp.concatenate([piece[:, j * out : (j + 1) * out] for piece in pieces], axis=1)
                for j in range(pack)
            ],
            axis=0,
        )
        return hidden + biases[layer : layer + 1]

    keep(first, norm_silu(inputs, gains[0:1]))
    toks = owner_of.shape[1]
    before = lax.broadcasted_iota(jnp.int32, (toks, toks), 0)
    after = lax.broadcasted_iota(jnp.int32, (toks, toks), 1)
    owner = owner_of[...]
    owner_column = jnp.sum(jnp.where(before == after, owner, 0), axis=1, keepdims=True)
    same = (owner_column == owner) & (before < after)
    rank = jnp.sum(jnp.where(same, 1, 0), axis=0, keepdims=True)
    slots = lax.broadcasted_iota(jnp.int32, (owners * SUBLANES, toks), 0)
    placing[...] = jnp.where(slots == owner * SUBLANES + rank, 1.0, 0.0).astype(jnp.bfloat16)
    pl.semaphore_wait(barrier, owners - 1)
    spread(first, 0)
    weight_copy.wait()
    hidden = convolve(first, 0)
    keep(second, norm_silu(hidden, gains[1:2]))
    spread(second, 1)
    hidden = convolve(second, 1)
    merged = feat[...].reshape(cells, width).astype(jnp.float32) + hidden
    active = norm_silu(merged, gains[2:3]).astype(jnp.bfloat16)
    rest = jnp.zeros((LANES - 4 * width_latent, width), jnp.bfloat16)
    latent_wide = jnp.concatenate([latent_rows[...]] * 4 + [rest], axis=0)
    latent = lax.dot_general(
        active, latent_wide, (((1,), (1,)), ((), ())), preferred_element_type=jnp.float32
    )
    cell = lax.broadcasted_iota(jnp.int32, (cells, LANES), 0)
    lane = lax.broadcasted_iota(jnp.int32, (cells, LANES), 1)
    corner = (cell // cols % 2) * 2 + cell % 2
    alive = (t * frames + cell // (rows * cols) < count[0]) & (corner == 0)
    flagged = jnp.where((lane == 4 * width_latent) & alive, 1.0, 0.0)
    patches = jnp.where(lane // width_latent == corner, latent, flagged).astype(jnp.bfloat16)
    spot = lax.broadcasted_iota(jnp.int32, (toks, cells), 1)
    patch = (spot // (2 * cols)) * (cols // 2) + spot % cols // 2
    mine = patch == lax.broadcasted_iota(jnp.int32, (toks, cells), 0)
    patches = jnp.dot(
        jnp.where(mine, 1.0, 0.0).astype(jnp.bfloat16), patches, preferred_element_type=jnp.float32
    ).astype(jnp.bfloat16)
    outgoing = jnp.dot(
        placing[...], patches, preferred_element_type=jnp.float32
    ).astype(jnp.bfloat16)
    tok_out[...] = outgoing.reshape(owners, SUBLANES, LANES)
    tok_in[pl.ds(me, 1)] = tok_out[pl.ds(me, 1)]

    def tok_copy(source, target):
        return pltpu.make_async_remote_copy(
            src_ref=tok_out.at[target], dst_ref=tok_in.at[source],
            send_sem=tok_send.at[target], recv_sem=tok_recv.at[source],
            device_id={"tm": target // ns, "space": target % ns}, device_id_type=MESH,
        )

    def tok_start(d, carry):
        tok_copy(me, (me + d) % owners).start()
        return carry

    def tok_wait(d, carry):
        o = (me + d) % owners
        tok_copy(o, o).wait_recv()
        return carry

    def tok_sent(d, carry):
        tok_copy(me, (me + d) % owners).wait_send()
        return carry

    lax.fori_loop(1, owners, tok_start, 0)
    spread_sent(first, 0)
    spread_sent(second, 1)
    lax.fori_loop(1, owners, tok_wait, 0)
    row = lax.broadcasted_iota(jnp.int32, (owners * most, owners * SUBLANES), 0)
    held = lax.broadcasted_iota(jnp.int32, (owners * most, owners * SUBLANES), 1)
    inner = held % SUBLANES
    chosen = (row == held // SUBLANES * most + inner) & (inner < most)
    tokens_out[...] = jnp.dot(
        jnp.where(chosen, 1.0, 0.0).astype(jnp.bfloat16),
        tok_in[...].reshape(owners * SUBLANES, LANES),
        preferred_element_type=jnp.float32,
    ).astype(jnp.bfloat16)
    lax.fori_loop(1, owners, tok_sent, 0)


def embedder(channels, tokens, weight, bias, packed):
    held = tokens[...]
    projected = jnp.dot(held[:, :channels], weight[...], preferred_element_type=jnp.float32)
    flags = held[:, channels : channels + 1].astype(jnp.float32)
    packed[...] = ((projected + bias[...]) * flags).astype(jnp.bfloat16)


def shards(
    features,
    frame_counts,
    routes,
    norm_gains,
    conv_weights,
    conv_biases,
    latent_weight,
    embed_weight,
    embed_bias,
):
    feat = features[0]
    frames, rows, cols, width = feat.shape
    cells = frames * rows * cols
    n, ns = lax.axis_size("tm"), lax.axis_size("space")
    owners = n * ns
    out = conv_weights.shape[1]
    pack = max(1, LANES // out)
    latents = latent_weight.shape[1]
    tok_count = routes.shape[1]
    most = (tok_count + owners - 1) // owners + 1
    vmem = pl.BlockSpec(memory_space=pltpu.VMEM)
    dma = pltpu.SemaphoreType.DMA
    field = pltpu.VMEM((n * frames + 2, rows + 2, cols, width), jnp.bfloat16)
    slab = pltpu.VMEM((2, n, cells // pack, pack * out), jnp.bfloat16)
    cuts = CUTS if frames % CUTS == 0 else 1
    tok = pltpu.VMEM((owners, SUBLANES, LANES), jnp.bfloat16)
    tokens = pl.pallas_call(
        functools.partial(encoder, n, ns, most, latents),
        out_shape=jax.ShapeDtypeStruct((owners * most, LANES), jnp.bfloat16),
        in_specs=[vmem, pl.BlockSpec(memory_space=pl.ANY), vmem, vmem, vmem, vmem,
                  pl.BlockSpec(memory_space=pltpu.SMEM)],
        out_specs=vmem,
        scratch_shapes=[
            field, field,
            pltpu.VMEM((2, 9, 3 * out, width), jnp.bfloat16),
            pltpu.VMEM((owners * SUBLANES, tok_count), jnp.bfloat16),
            slab, slab, tok, tok,
            dma,
            dma((2, 2, n, cuts)), dma((2, n, cuts)), dma((2, n, cuts)), dma((2, n, cuts)),
            dma((2, n, cuts)), dma((2, n, cuts)),
            dma((2, n)), dma((2, n)), dma((owners,)), dma((owners,)),
        ],
        compiler_params=pltpu.CompilerParams(collective_id=0, has_side_effects=True),
    )(
        feat,
        conv_weights.transpose(0, 2, 1, 3).reshape(2, 9, 3 * out, width),
        norm_gains,
        conv_biases,
        latent_weight.T,
        routes.reshape(1, tok_count),
        frame_counts,
    )
    channels = 4 * latents
    embed = embed_weight.shape[1]
    chunk = embed // 1 if embed % (1 * LANES) == 0 else embed
    packed = pl.pallas_call(
        functools.partial(embedder, channels),
        grid=(embed // chunk,),
        out_shape=jax.ShapeDtypeStruct((owners * most, embed), jnp.bfloat16),
        in_specs=[
            pl.BlockSpec((owners * most, LANES), lambda i: (0, 0)),
            pl.BlockSpec((channels, chunk), lambda i: (0, i)),
            pl.BlockSpec((1, chunk), lambda i: (0, i)),
        ],
        out_specs=pl.BlockSpec((owners * most, chunk), lambda i: (0, i)),
    )(tokens, embed_weight, embed_bias.reshape(1, embed))
    return packed[None]


def solution(mesh):
    return jax.shard_map(
        shards,
        mesh=mesh,
        in_specs=(
            P(("groups", "clip"), "tm", "space", None, None),
            P(("groups", "clip")),
            P(("groups", "clip"), ("tm", "space"), None),
            P(),
            P(None, "tm", None, None),
            P(),
            P(),
            P(),
            P(),
        ),
        out_specs=P(("groups", "clip"), ("tm", "space"), None),
        check_vma=False,
    )
```

profile of v0, /device:TPU:0, one launch (start us, length us, event | category | flops | bytes accessed | tf_op | source)
XLA Modules:
  0.0 52.1 jit_solution(14910934376203926105)
XLA Ops:
  0.7 49.4 %shard_map.91.tokens = bf16[72,128]{1,0:T(8,128)(2,1)} custom-call(bf16[4,4,16,256]{3,2,1,0:T(8,128)(2,1)} %bitcast.9, bf16[2,9,192,256]{3,2,1,0:T(8,128)(2,1)} %bitcast.8, f32[3,256]{1,0:T(4,128)} %gains.1, f32[2,256]{1,0:T(2,128)} %biases.1, bf16[16,256]{1,0:T(8,128)(2,1)} %bitcast.11, s32[1,64]{1,0:T(1,128)} %bitcast.12, s32[1]{0:T(128)S(6)} %copy.10.count), custom_call_target="tpu_custom_call" | custom-call | tf_op jit(solution)/shard_map/pallas_call | solution.py:313
  50.0 2.0 %shard_map.92 = bf16[72,3072]{1,0:T(8,128)(2,1)} custom-call(bf16[72,128]{1,0:T(8,128)(2,1)} %shard_map.91.tokens, bf16[64,3072]{1,0:T(8,128)(2,1)} %weight.1, f32[1,3072]{1,0:T(1,128)} %bitcast.10), custom_call_target="tpu_custom_call" | custom-call | tf_op jit(solution)/shard_map/pallas_call | solution.py:342
where the time goes:
time: 52.2 us; the launch traced here: 52.1 us
  Pallas kernels  51.4 us (98%)
  between operations  0.66 us (1%)
    pallas_call x1, Pallas kernels, shards(): pl.pallas_call(functools.partial(encoder, n, ns, most, latents), out_shap...  49.4 us
    pallas_call x1, Pallas kernels, shards(): pl.pallas_call(functools.partial(embedder, channels), grid=(embed // chun...  2.03 us

commit v1 on v0

v1 whole, which is shorter than its diff:
```python
import functools

import jax
import jax.numpy as jnp
from jax import lax
from jax.experimental import pallas as pl
from jax.experimental.pallas import tpu as pltpu
from jax.sharding import PartitionSpec as P

MESH = pl.DeviceIdType.MESH
LANES = 128
SUBLANES = 16
CUTS = 4


def norm_silu(values, gain):
    scale = lax.rsqrt(jnp.mean(values * values, axis=-1, keepdims=True) + 1e-06)
    scaled = values * scale * gain
    return scaled / (1.0 + jnp.exp(-scaled))


def encoder(
    n, ns, most, width_latent,
    feat, weights_any, gains, biases, latent_rows, owner_of, count,
    tokens_out,
    field, taps, placing, slab_out, slab_in, edge_out, edge_in, tok_out, tok_in,
    raw_sem, block_send, relay_send, block_recv,
    slab_send, slab_recv, edge_send, edge_recv, tok_send, tok_recv,
):
    t = lax.axis_index("tm")
    s = lax.axis_index("space")
    me = t * ns + s
    owners = n * ns
    frames, rows, cols, width = feat.shape
    cells = frames * rows * cols
    out = weights_any.shape[2] // 3
    cuts = block_recv.shape[2]
    size = frames // cuts
    pack = max(1, LANES // out)
    relays = n == 4

    barrier = pltpu.get_barrier_semaphore()

    def greet(d, carry):
        o = (me + d) % owners
        pl.semaphore_signal(
            barrier, inc=1, device_id={"tm": o // ns, "space": o % ns}, device_id_type=MESH
        )
        return carry

    lax.fori_loop(1, owners, greet, 0)
    weight_copy = pltpu.make_async_copy(weights_any, taps, raw_sem)
    weight_copy.start()

    field[:, 0:2] = jnp.zeros((2, 2) + field.shape[2:], field.dtype)

    @pl.when(s == 0)
    def _():
        edge_in[:, 0] = jnp.zeros((2,) + edge_in.shape[2:], edge_in.dtype)

    @pl.when(s == ns - 1)
    def _():
        edge_in[:, 1] = jnp.zeros((2,) + edge_in.shape[2:], edge_in.dtype)

    inputs = feat[...].reshape(cells, width).astype(jnp.float32)

    def keep(layer, active):
        field[layer, pl.ds(2 + frames * t, frames)] = active.astype(jnp.bfloat16).reshape(
            frames, rows, cols, width
        )

    def block_copy(layer, c, f, target, send_sem):
        span = field.at[layer, pl.ds(2 + frames * c + size * f, size)]
        return pltpu.make_async_remote_copy(
            src_ref=span, dst_ref=span, send_sem=send_sem, recv_sem=block_recv.at[layer, c, f],
            device_id={"tm": target}, device_id_type=MESH,
        )

    def slab_copy(layer, source, target):
        return pltpu.make_async_remote_copy(
            src_ref=slab_out.at[layer, target], dst_ref=slab_in.at[layer, source],
            send_sem=slab_send.at[layer, target], recv_sem=slab_recv.at[layer, source],
            device_id={"tm": target}, device_id_type=MESH,
        )

    def edge_copy(layer, side, source, target):
        return pltpu.make_async_remote_copy(
            src_ref=edge_out.at[layer, side, target], dst_ref=edge_in.at[layer, side, source],
            send_sem=edge_send.at[layer, side, target], recv_sem=edge_recv.at[layer, side, source],
            device_id={"tm": target, "space": (s + 1 - 2 * side + ns) % ns}, device_id_type=MESH,
        )

    def sided(side, act):
        pl.when(s < ns - 1 if side == 0 else s > 0)(act)

    def fed(side, act):
        pl.when(s > 0 if side == 0 else s < ns - 1)(act)

    def targets(layer, act):
        for d in range(n - 1, 0, -1):
            for target in (t - d, t + d):
                here = (target >= 0) & (target < n)
                if relays and d == 2:
                    here = here & ((t == 0) | (t == n - 1))
                spot = (target + n) % n

                def each(spot=spot):
                    for f in range(cuts):
                        act(block_copy(layer, t, f, spot, block_send.at[layer, spot, f]))

                pl.when(here)(each)

    def far_targets(layer, act):
        def each(d, carry):
            spot = (t + d) % n
            for f in range(cuts):
                act(block_copy(layer, t, f, spot, block_send.at[layer, spot, f]))
            return carry

        lax.fori_loop(1, n, each, 0)

    reach = targets if n <= 8 else far_targets
    relay_target = jnp.where(t == 1, 0, n - 1)
    relay_source = jnp.where(t == 1, 2, 1)

    def relay_copy(layer, f):
        return block_copy(layer, relay_source, f, relay_target, relay_send.at[layer, f])

    def sent(layer):
        reach(layer, lambda copy: copy.wait_send())
        if relays:

            @pl.when((t == 1) | (t == 2))
            def _():
                for f in range(cuts):
                    relay_copy(layer, f).wait_send()

        def each(c, carry):
            pl.when(c != t)(lambda: slab_copy(layer, t, c).wait_send())
            for side in range(2):
                sided(side, lambda: edge_copy(layer, side, t, c).wait_send())
            return carry

        lax.fori_loop(0, n, each, 0)

    def arrived(layer, c):
        for f in range(cuts):
            block_copy(layer, c, f, c, block_send.at[layer, c, f]).wait_recv()

    def arrived_relay(layer, c):
        for f in range(cuts):
            block_copy(layer, c, f, c, block_send.at[layer, c, f]).wait_recv()
            relay_copy(layer, f).start()

    grid_rows = rows + 2
    column = lax.broadcasted_iota(jnp.int32, (frames * grid_rows * cols, 1), 0) % cols

    def fold(values):
        part = values.shape[0] // pack
        return jnp.concatenate([values[j * part : (j + 1) * part] for j in range(pack)], axis=1)

    def unfold(pieces):
        return jnp.concatenate(
            [
                jnp.concatenate([piece[:, j * out : (j + 1) * out] for piece in pieces], axis=1)
                for j in range(pack)
            ],
            axis=0,
        )

    def convolve(layer):
        def one(b):
            sums = []
            for r in range(3):
                total = None
                for a in range(3):
                    block = field[layer, pl.ds(frames * b + a, frames)]
                    term = lax.dot_general(
                        block.reshape(cells, width), taps[layer, 3 * a + r],
                        (((1,), (1,)), ((), ())), preferred_element_type=jnp.float32,
                    )
                    total = term if total is None else total + term
                sums.append(total.reshape(frames, rows, cols, 3 * out))
            blank = jnp.zeros((frames, 1, cols, 3 * out), jnp.float32)
            two = jnp.concatenate([blank] * 2, axis=1)
            wide = (
                jnp.concatenate([sums[2], two], axis=1)
                + jnp.concatenate([blank, sums[1], blank], axis=1)
                + jnp.concatenate([two, sums[0]], axis=1)
            ).reshape(frames * grid_rows * cols, 3 * out)
            last = frames * grid_rows * cols - 1
            left = jnp.where(column == 0, 0.0, pltpu.roll(wide[:, :out], 1, 0))
            right = jnp.where(column == cols - 1, 0.0, pltpu.roll(wide[:, 2 * out :], last, 0))
            summed = (left + wide[:, out : 2 * out] + right).reshape(frames, grid_rows, cols, out)
            inner = summed[:, 1 : rows + 1].reshape(cells, out)
            edges = (
                summed[:, rows + 1 :].reshape(frames * cols, out),
                summed[:, :1].reshape(frames * cols, out),
            )
            packed = fold(inner).astype(jnp.bfloat16)

            @pl.when(b == t)
            def _():
                slab_in[layer, pl.ds(t, 1)] = packed[None]

            @pl.when(b != t)
            def _():
                slab_out[layer, pl.ds(b, 1)] = packed[None]
                slab_copy(layer, t, b).start()

            for side in range(2):

                def give(side=side):
                    edge_out[layer, side, pl.ds(b, 1)] = fold(edges[side]).astype(jnp.bfloat16)[None]
                    edge_copy(layer, side, t, b).start()

                sided(side, give)

        if relays:
            order = ((0, 1, 3, 2), (2, 3, 0, 1), (2, 0, 1, 3), (0, 3, 1, 2))
            needs = (
                ((), (1,), (3, 2), ()),
                ((2,), (3,), (0,), ()),
                ((1,), (0,), (), (3,)),
                ((0,), (2,), (1,), ()),
            )

            def pick(k):
                spot = order[0][k]
                for i in range(1, n):
                    spot = jnp.where(t == i, order[i][k], spot)
                return spot

            for i in range(n):
                if needs[i][0]:
                    wait = arrived_relay if i in (1, 2) else arrived
                    pl.when(t == i)(functools.partial(wait, layer, needs[i][0][0]))

            def step(k, carry):
                for i in range(n):
                    for kk in range(1, n):
                        for c in needs[i][kk]:
                            pl.when((t == i) & (k == kk))(functools.partial(arrived, layer, c))
                spot = pick(0)
                for kk in range(1, n):
                    spot = jnp.where(k == kk, pick(kk), spot)
                one(spot)
                return carry

            lax.fori_loop(0, n, step, 0)
        else:

            def hold(d, carry):
                arrived(layer, (t + d) % n)
                return carry

            lax.fori_loop(1, n, hold, 0)

            def step(d, carry):
                one((t + d) % n)
                return carry

            lax.fori_loop(1, n + 1, step, 0)

        def came(k, carry):
            q = (t + k) % n
            pl.when(k > 0)(lambda: slab_copy(layer, q, q).wait_recv())
            for side in range(2):
                fed(side, lambda: edge_copy(layer, side, q, q).wait_recv())
            return carry

        lax.fori_loop(0, n, came, 0)
        hidden = unfold([slab_in[layer, q].astype(jnp.float32) for q in range(n)])
        top, low = [
            unfold([edge_in[layer, side, q].astype(jnp.float32) for q in range(n)]).reshape(
                frames, 1, cols, width
            )
            for side in range(2)
        ]
        hidden = hidden.reshape(frames, rows, cols, width)
        if rows > 1:
            hidden = jnp.concatenate(
                [hidden[:, :1] + top, hidden[:, 1 : rows - 1], hidden[:, rows - 1 :] + low], axis=1
            )
        else:
            hidden = hidden + top + low
        return hidden.reshape(cells, width) + biases[layer : layer + 1]

    keep(0, norm_silu(inputs, gains[0:1]))
    toks = owner_of.shape[1]
    before = lax.broadcasted_iota(jnp.int32, (toks, toks), 0)
    after = lax.broadcasted_iota(jnp.int32, (toks, toks), 1)
    owner = owner_of[...]
    owner_column = jnp.sum(jnp.where(before == after, owner, 0), axis=1, keepdims=True)
    same = (owner_column == owner) & (before < after)
    rank = jnp.sum(jnp.where(same, 1, 0), axis=0, keepdims=True)
    slots = lax.broadcasted_iota(jnp.int32, (owners * SUBLANES, toks), 0)
    placing[...] = jnp.where(slots == owner * SUBLANES + rank, 1.0, 0.0).astype(jnp.bfloat16)
    pl.semaphore_wait(barrier, owners - 1)
    reach(0, lambda copy: copy.start())
    weight_copy.wait()
    hidden = convolve(0)
    keep(1, norm_silu(hidden, gains[1:2]))
    reach(1, lambda copy: copy.start())
    hidden = convolve(1)
    merged = feat[...].reshape(cells, width).astype(jnp.float32) + hidden
    active = norm_silu(merged, gains[2:3]).astype(jnp.bfloat16)
    rest = jnp.zeros((LANES - 4 * width_latent, width), jnp.bfloat16)
    latent_wide = jnp.concatenate([latent_rows[...]] * 4 + [rest], axis=0)
    latent = lax.dot_general(
        active, latent_wide, (((1,), (1,)), ((), ())), preferred_element_type=jnp.float32
    )
    cell = lax.broadcasted_iota(jnp.int32, (cells, LANES), 0)
    lane = lax.broadcasted_iota(jnp.int32, (cells, LANES), 1)
    corner = (cell // cols % 2) * 2 + cell % 2
    alive = (t * frames + cell // (rows * cols) < count[0]) & (corner == 0)
    flagged = jnp.where((lane == 4 * width_latent) & alive, 1.0, 0.0)
    patches = jnp.where(lane // width_latent == corner, latent, flagged).astype(jnp.bfloat16)
    spot = lax.broadcasted_iota(jnp.int32, (toks, cells), 1)
    patch = (spot // (2 * cols)) * (cols // 2) + spot % cols // 2
    mine = patch == lax.broadcasted_iota(jnp.int32, (toks, cells), 0)
    patches = jnp.dot(
        jnp.where(mine, 1.0, 0.0).astype(jnp.bfloat16), patches, preferred_element_type=jnp.float32
    ).astype(jnp.bfloat16)
    outgoing = jnp.dot(
        placing[...], patches, preferred_element_type=jnp.float32
    ).astype(jnp.bfloat16)
    tok_out[...] = outgoing.reshape(owners, SUBLANES, LANES)
    tok_in[pl.ds(me, 1)] = tok_out[pl.ds(me, 1)]

    def tok_copy(source, target):
        return pltpu.make_async_remote_copy(
            src_ref=tok_out.at[target], dst_ref=tok_in.at[source],
            send_sem=tok_send.at[target], recv_sem=tok_recv.at[source],
            device_id={"tm": target // ns, "space": target % ns}, device_id_type=MESH,
        )

    def tok_start(d, carry):
        tok_copy(me, (me + d) % owners).start()
        return carry

    def tok_wait(d, carry):
        o = (me + d) % owners
        tok_copy(o, o).wait_recv()
        return carry

    def tok_sent(d, carry):
        tok_copy(me, (me + d) % owners).wait_send()
        return carry

    lax.fori_loop(1, owners, tok_start, 0)
    sent(0)
    sent(1)
    lax.fori_loop(1, owners, tok_wait, 0)
    row = lax.broadcasted_iota(jnp.int32, (owners * most, owners * SUBLANES), 0)
    held = lax.broadcasted_iota(jnp.int32, (owners * most, owners * SUBLANES), 1)
    inner = held % SUBLANES
    chosen = (row == held // SUBLANES * most + inner) & (inner < most)
    tokens_out[...] = jnp.dot(
        jnp.where(chosen, 1.0, 0.0).astype(jnp.bfloat16),
        tok_in[...].reshape(owners * SUBLANES, LANES),
        preferred_element_type=jnp.float32,
    ).astype(jnp.bfloat16)
    lax.fori_loop(1, owners, tok_sent, 0)


def embedder(channels, tokens, weight, bias, packed):
    held = tokens[...]
    projected = jnp.dot(held[:, :channels], weight[...], preferred_element_type=jnp.float32)
    flags = held[:, channels : channels + 1].astype(jnp.float32)
    packed[...] = ((projected + bias[...]) * flags).astype(jnp.bfloat16)


def shards(
    features,
    frame_counts,
    routes,
    norm_gains,
    conv_weights,
    conv_biases,
    latent_weight,
    embed_weight,
    embed_bias,
):
    feat = features[0]
    frames, rows, cols, width = feat.shape
    cells = frames * rows * cols
    n, ns = lax.axis_size("tm"), lax.axis_size("space")
    owners = n * ns
    out = conv_weights.shape[1]
    pack = max(1, LANES // out)
    latents = latent_weight.shape[1]
    tok_count = routes.shape[1]
    most = (tok_count + owners - 1) // owners + 1
    vmem = pl.BlockSpec(memory_space=pltpu.VMEM)
    dma = pltpu.SemaphoreType.DMA
    field = pltpu.VMEM((2, n * frames + 2, rows, cols, width), jnp.bfloat16)
    slab = pltpu.VMEM((2, n, cells // pack, pack * out), jnp.bfloat16)
    edge = pltpu.VMEM((2, 2, n, frames * cols // pack, pack * out), jnp.bfloat16)
    cuts = CUTS if frames % CUTS == 0 else 1
    tok = pltpu.VMEM((owners, SUBLANES, LANES), jnp.bfloat16)
    tokens = pl.pallas_call(
        functools.partial(encoder, n, ns, most, latents),
        out_shape=jax.ShapeDtypeStruct((owners * most, LANES), jnp.bfloat16),
        in_specs=[vmem, pl.BlockSpec(memory_space=pl.ANY), vmem, vmem, vmem, vmem,
                  pl.BlockSpec(memory_space=pltpu.SMEM)],
        out_specs=vmem,
        scratch_shapes=[
            field,
            pltpu.VMEM((2, 9, 3 * out, width), jnp.bfloat16),
            pltpu.VMEM((owners * SUBLANES, tok_count), jnp.bfloat16),
            slab, slab, edge, edge, tok, tok,
            dma,
            dma((2, n, cuts)), dma((2, cuts)), dma((2, n, cuts)),
            dma((2, n)), dma((2, n)), dma((2, 2, n)), dma((2, 2, n)),
            dma((owners,)), dma((owners,)),
        ],
        compiler_params=pltpu.CompilerParams(collective_id=0, has_side_effects=True),
    )(
        feat,
        conv_weights.transpose(0, 2, 1, 3).reshape(2, 9, 3 * out, width),
        norm_gains,
        conv_biases,
        latent_weight.T,
        routes.reshape(1, tok_count),
        frame_counts,
    )
    channels = 4 * latents
    embed = embed_weight.shape[1]
    chunk = embed // 1 if embed % (1 * LANES) == 0 else embed
    packed = pl.pallas_call(
        functools.partial(embedder, channels),
        grid=(embed // chunk,),
        out_shape=jax.ShapeDtypeStruct((owners * most, embed), jnp.bfloat16),
        in_specs=[
            pl.BlockSpec((owners * most, LANES), lambda i: (0, 0)),
            pl.BlockSpec((channels, chunk), lambda i: (0, i)),
            pl.BlockSpec((1, chunk), lambda i: (0, i)),
        ],
        out_specs=pl.BlockSpec((owners * most, chunk), lambda i: (0, i)),
    )(tokens, embed_weight, embed_bias.reshape(1, embed))
    return packed[None]


def solution(mesh):
    return jax.shard_map(
        shards,
        mesh=mesh,
        in_specs=(
            P(("groups", "clip"), "tm", "space", None, None),
            P(("groups", "clip")),
            P(("groups", "clip"), ("tm", "space"), None),
            P(),
            P(None, "tm", None, None),
            P(),
            P(),
            P(),
            P(),
        ),
        out_specs=P(("groups", "clip"), ("tm", "space"), None),
        check_vma=False,
    )
```

time: 52.2 us -> 52.7 us (level)
  no operation moved by 1% of the time
where the time goes in v1:
time: 52.7 us; the launch traced here: 52.5 us
  Pallas kernels  51.8 us (98%)
  between operations  0.66 us (1%)
    pallas_call x1, Pallas kernels, shards(): pl.pallas_call(functools.partial(encoder, n, ns, most, latents), out_shap...  49.8 us
    pallas_call x1, Pallas kernels, shards(): pl.pallas_call(functools.partial(embedder, channels), grid=(embed // chun...  2.03 us

profile of v1, /device:TPU:0, one launch (start us, length us, event | category | flops | bytes accessed | tf_op | source)
XLA Modules:
  0.0 52.5 jit_solution(6193104813388121148)
XLA Ops:
  0.7 49.8 %shard_map.91.tokens = bf16[72,128]{1,0:T(8,128)(2,1)} custom-call(bf16[4,4,16,256]{3,2,1,0:T(8,128)(2,1)} %bitcast.9, bf16[2,9,192,256]{3,2,1,0:T(8,128)(2,1)} %bitcast.8, f32[3,256]{1,0:T(4,128)} %gains.1, f32[2,256]{1,0:T(2,128)} %biases.1, bf16[16,256]{1,0:T(8,128)(2,1)} %bitcast.11, s32[1,64]{1,0:T(1,128)} %bitcast.12, s32[1]{0:T(128)S(6)} %copy.10.count), custom_call_target="tpu_custom_call" | custom-call | tf_op jit(solution)/shard_map/pallas_call | solution.py:402
  50.5 2.0 %shard_map.92 = bf16[72,3072]{1,0:T(8,128)(2,1)} custom-call(bf16[72,128]{1,0:T(8,128)(2,1)} %shard_map.91.tokens, bf16[64,3072]{1,0:T(8,128)(2,1)} %weight.1, f32[1,3072]{1,0:T(1,128)} %bitcast.10), custom_call_target="tpu_custom_call" | custom-call | tf_op jit(solution)/shard_map/pallas_call | solution.py:431

commit v2 on v0

v2 whole, which is shorter than its diff:
```python
import functools

import jax
import jax.numpy as jnp
from jax import lax
from jax.experimental import pallas as pl
from jax.experimental.pallas import tpu as pltpu
from jax.sharding import PartitionSpec as P

MESH = pl.DeviceIdType.MESH
LANES = 128
SUBLANES = 16
CUTS = 4


def norm_silu(values, gain):
    scale = lax.rsqrt(jnp.mean(values * values, axis=-1, keepdims=True) + 1e-06)
    scaled = values * scale * gain
    return scaled / (1.0 + jnp.exp(-scaled))


def encoder(
    n, ns, ng, nc, most, width_latent,
    feat, weights_any, shares_any, gains, biases, latent_rows, owner_of, count,
    tokens_out,
    field, inner, taps, shares, placing, slab_out, slab_in, edge_out, edge_in, tok_out, tok_in,
    raw_sem, share_sem, block_send, relay_send, block_recv,
    slab_send, slab_recv, edge_send, edge_recv, halo_send, halo_recv,
    line_send, line_relay, line_recv, plane_send, plane_recv, core_send, core_recv,
    tok_send, tok_recv,
):
    t = lax.axis_index("tm")
    s = lax.axis_index("space")
    g = lax.axis_index("groups")
    core = lax.axis_index("clip")
    me = t * ns + s
    owners = n * ns
    frames, rows, cols, width = feat.shape
    cells = frames * rows * cols
    out = weights_any.shape[2] // 3
    cuts = block_recv.shape[1]
    size = frames // cuts
    pack = max(1, LANES // out)
    relays = n == 4
    columns, parts, _, share_rows, share_lanes = shares.shape[1:]
    shared = columns > 1
    column_of = g * ns + s if shared else 0
    part_of = core if shared else 0

    barrier = pltpu.get_barrier_semaphore()

    def greet(d, carry):
        o = (me + d) % owners
        pl.semaphore_signal(
            barrier, inc=1, device_id={"tm": o // ns, "space": o % ns}, device_id_type=MESH
        )
        return carry

    lax.fori_loop(1, owners, greet, 0)
    expected = owners - 1
    if shared:
        for dg in range(1, ng):
            for other in range(ns):
                pl.semaphore_signal(
                    barrier, inc=1, device_id={"groups": (g + dg) % ng, "space": other},
                    device_id_type=MESH,
                )
                expected += 1
        for dc in range(1, nc):
            pl.semaphore_signal(
                barrier, inc=1, device_id={"clip": (core + dc) % nc}, device_id_type=MESH
            )
            expected += 1
    weight_copy = pltpu.make_async_copy(weights_any.at[0], taps, raw_sem)

    def share_load(col, part):
        lanes = pl.ds(pl.multiple_of(part * share_lanes, LANES), share_lanes)
        return pltpu.make_async_copy(
            shares_any.at[1, :, pl.ds(col * share_rows, share_rows), lanes],
            shares.at[t, col, part], share_sem.at[col, part],
        )

    share_load(column_of, part_of).start()
    weight_copy.start()

    def others(act):
        for col in range(columns):
            for part in range(parts):
                pl.when((column_of != col) | (part_of != part))(lambda: act(share_load(col, part)))

    others(lambda copy: copy.start())

    field[0:2] = jnp.zeros((2,) + field.shape[1:], field.dtype)

    @pl.when(t == 0)
    def _():
        inner[0:2] = jnp.zeros((2,) + inner.shape[1:], inner.dtype)

    @pl.when(s == 0)
    def _():
        edge_in[0] = jnp.zeros(edge_in.shape[1:], edge_in.dtype)
        inner[:, 0:1] = jnp.zeros((inner.shape[0], 1) + inner.shape[2:], inner.dtype)

    @pl.when(s == ns - 1)
    def _():
        edge_in[1] = jnp.zeros(edge_in.shape[1:], edge_in.dtype)
        inner[:, rows + 1 :] = jnp.zeros((inner.shape[0], 1) + inner.shape[2:], inner.dtype)

    inputs = feat[...].reshape(cells, width).astype(jnp.float32)

    def block_copy(c, f, target, send_sem):
        span = field.at[pl.ds(2 + frames * c + size * f, size)]
        return pltpu.make_async_remote_copy(
            src_ref=span, dst_ref=span, send_sem=send_sem, recv_sem=block_recv.at[c, f],
            device_id={"tm": target}, device_id_type=MESH,
        )

    def slab_copy(source, target):
        return pltpu.make_async_remote_copy(
            src_ref=slab_out.at[target], dst_ref=slab_in.at[source],
            send_sem=slab_send.at[target], recv_sem=slab_recv.at[source],
            device_id={"tm": target}, device_id_type=MESH,
        )

    def edge_copy(side, source, target):
        return pltpu.make_async_remote_copy(
            src_ref=edge_out.at[side, target], dst_ref=edge_in.at[side, source],
            send_sem=edge_send.at[side, target], recv_sem=edge_recv.at[side, source],
            device_id={"tm": target, "space": (s + 1 - 2 * side + ns) % ns}, device_id_type=MESH,
        )

    def sided(side, act):
        pl.when(s < ns - 1 if side == 0 else s > 0)(act)

    def fed(side, act):
        pl.when(s > 0 if side == 0 else s < ns - 1)(act)

    def line_copy(q, target, send_sem):
        piece = shares.at[q, column_of, part_of]
        return pltpu.make_async_remote_copy(
            src_ref=piece, dst_ref=piece, send_sem=send_sem, recv_sem=line_recv.at[q],
            device_id={"tm": target}, device_id_type=MESH,
        )

    def plane_copy(q, col, d):
        piece = shares.at[q, col, part_of]
        peer = (column_of + d) % columns
        return pltpu.make_async_remote_copy(
            src_ref=piece, dst_ref=piece,
            send_sem=plane_send.at[q, d], recv_sem=plane_recv.at[q, col],
            device_id={"groups": peer // ns, "space": peer % ns}, device_id_type=MESH,
        )

    def core_copy(q, col, part, d):
        piece = shares.at[q, col, part]
        return pltpu.make_async_remote_copy(
            src_ref=piece, dst_ref=piece,
            send_sem=core_send.at[q, col, d], recv_sem=core_recv.at[q, col, part],
            device_id={"clip": (core + d) % nc}, device_id_type=MESH,
        )

    def along(first, act):
        for d in range(n - 1, 0, -1):
            if first is not None and (d == 1) != first:
                continue
            for target in (t - d, t + d):
                here = (target >= 0) & (target < n)
                if relays and d == 2:
                    here = here & ((t == 0) | (t == n - 1))
                pl.when(here)(functools.partial(act, (target + n) % n))

    def around(act):
        def each(d, carry):
            act((t + d) % n)
            return carry

        lax.fori_loop(1, n, each, 0)

    small = n <= 8

    def blocks(act):
        def each(spot):
            for f in range(cuts):
                act(block_copy(t, f, spot, block_send.at[spot, f]))

        along(None, each) if small else around(each)

    def line_of(act):
        return lambda spot: act(line_copy(t, spot, line_send.at[spot]))

    relay_target = jnp.where(t == 1, 0, n - 1)
    relay_source = jnp.where(t == 1, 2, 1)
    relaying = (t == 1) | (t == 2)

    def relay_copy(f):
        return block_copy(relay_source, f, relay_target, relay_send.at[f])

    def line_relay_copy():
        return line_copy(relay_source, relay_target, line_relay)

    def pass_on(q):
        line_copy(q, q, line_send.at[q]).wait_recv()
        if shared:
            for d in range(1, columns):
                plane_copy(q, column_of, d).start()
            for d in range(1, nc):
                core_copy(q, column_of, part_of, d).start()

    def cross(q):
        for d in range(1, columns):
            col = (column_of + d) % columns
            plane_copy(q, col, d).wait_recv()
            for dc in range(1, nc):
                core_copy(q, col, part_of, dc).start()

    def arrived(c):
        for f in range(cuts):
            block_copy(c, f, c, block_send.at[c, f]).wait_recv()

    grid_rows = rows + 2
    column = lax.broadcasted_iota(jnp.int32, (frames * grid_rows * cols, 1), 0) % cols

    def fold(values):
        part = values.shape[0] // pack
        return jnp.concatenate([values[j * part : (j + 1) * part] for j in range(pack)], axis=1)

    def unfold(pieces):
        return jnp.concatenate(
            [
                jnp.concatenate([piece[:, j * out : (j + 1) * out] for piece in pieces], axis=1)
                for j in range(pack)
            ],
            axis=0,
        )

    def beside(left, middle, right):
        count = left.shape[0]
        mark = column[:count]
        left = jnp.where(mark == 0, 0.0, pltpu.roll(left, 1, 0))
        right = jnp.where(mark == cols - 1, 0.0, pltpu.roll(right, count - 1, 0))
        return left + middle + right

    def one(b):
        sums = []
        for r in range(3):
            total = None
            for a in range(3):
                block = field[pl.ds(frames * b + a, frames)]
                term = lax.dot_general(
                    block.reshape(cells, width), taps[3 * a + r],
                    (((1,), (1,)), ((), ())), preferred_element_type=jnp.float32,
                )
                total = term if total is None else total + term
            sums.append(total.reshape(frames, rows, cols, 3 * out))
        blank = jnp.zeros((frames, 1, cols, 3 * out), jnp.float32)
        two = jnp.concatenate([blank] * 2, axis=1)
        wide = (
            jnp.concatenate([sums[2], two], axis=1)
            + jnp.concatenate([blank, sums[1], blank], axis=1)
            + jnp.concatenate([two, sums[0]], axis=1)
        ).reshape(frames * grid_rows * cols, 3 * out)
        summed = beside(wide[:, :out], wide[:, out : 2 * out], wide[:, 2 * out :])
        summed = summed.reshape(frames, grid_rows, cols, out)
        edges = (
            summed[:, rows + 1 :].reshape(frames * cols, out),
            summed[:, :1].reshape(frames * cols, out),
        )
        packed = fold(summed[:, 1 : rows + 1].reshape(cells, out)).astype(jnp.bfloat16)

        @pl.when(b == t)
        def _():
            slab_in[pl.ds(t, 1)] = packed[None]

        @pl.when(b != t)
        def _():
            slab_out[pl.ds(b, 1)] = packed[None]
            slab_copy(t, b).start()

        for side in range(2):

            def give(side=side):
                edge_out[side, pl.ds(b, 1)] = fold(edges[side]).astype(jnp.bfloat16)[None]
                edge_copy(side, t, b).start()

            sided(side, give)

    def halo_copies(act):
        near, far = pl.ds(frames, 2), pl.ds(0, 2)
        own, body = pl.ds(2, frames), pl.ds(1, rows)
        up = {"tm": (t + 1) % n}
        more = t < n - 1

        def copy(i, here, source, target, device):
            pl.when(here)(
                lambda: act(
                    pltpu.make_async_remote_copy(
                        src_ref=inner.at[source], dst_ref=inner.at[target],
                        send_sem=halo_send.at[i], recv_sem=halo_recv.at[i],
                        device_id=device, device_id_type=MESH,
                    )
                )
            )

        left, right = {"space": (s + ns - 1) % ns}, {"space": (s + 1) % ns}
        first, last = pl.ds(1, 1), pl.ds(rows, 1)
        above, below = pl.ds(0, 1), pl.ds(rows + 1, 1)
        copy(0, more, (near, body), (far, body), up)
        copy(1, more & (s > 0), (near, first), (far, below), up | left)
        copy(2, more & (s < ns - 1), (near, last), (far, above), up | right)
        copy(3, s > 0, (own, first), (own, below), left)
        copy(4, s < ns - 1, (own, last), (own, above), right)

    def halo_came():
        def wait(i, here, target):
            def act():
                span = inner.at[target]
                pltpu.make_async_remote_copy(
                    src_ref=span, dst_ref=span, send_sem=halo_send.at[i],
                    recv_sem=halo_recv.at[i], device_id={"tm": t}, device_id_type=MESH,
                ).wait_recv()

            pl.when(here)(act)

        far, own, body = pl.ds(0, 2), pl.ds(2, frames), pl.ds(1, rows)
        above, below = pl.ds(0, 1), pl.ds(rows + 1, 1)
        wait(3, s < ns - 1, (own, below))
        wait(4, s > 0, (own, above))
        wait(0, t > 0, (far, body))
        wait(1, (t > 0) & (s < ns - 1), (far, below))
        wait(2, (t > 0) & (s > 0), (far, above))

    def kernel_of(tap):
        return jnp.concatenate(
            [
                jnp.concatenate([shares[q, col, part, tap] for part in range(parts)], axis=1)
                for q in range(n)
                for col in range(columns)
            ],
            axis=0,
        )

    field[pl.ds(2 + frames * t, frames)] = norm_silu(inputs, gains[0:1]).astype(
        jnp.bfloat16
    ).reshape(frames, rows, cols, width)
    toks = owner_of.shape[1]
    before = lax.broadcasted_iota(jnp.int32, (toks, toks), 0)
    after = lax.broadcasted_iota(jnp.int32, (toks, toks), 1)
    owner = owner_of[...]
    owner_column = jnp.sum(jnp.where(before == after, owner, 0), axis=1, keepdims=True)
    same = (owner_column == owner) & (before < after)
    rank = jnp.sum(jnp.where(same, 1, 0), axis=0, keepdims=True)
    slots = lax.broadcasted_iota(jnp.int32, (owners * SUBLANES, toks), 0)
    placing[...] = jnp.where(slots == owner * SUBLANES + rank, 1.0, 0.0).astype(jnp.bfloat16)
    share_load(column_of, part_of).wait()
    pl.semaphore_wait(barrier, expected)
    start = lambda copy: copy.start()
    if small:
        along(True, line_of(start))
        blocks(start)
        along(False, line_of(start))
    else:
        blocks(start)
        around(line_of(start))
    weight_copy.wait()
    if relays:
        order = ((0, 1, 3, 2), (2, 3, 0, 1), (2, 0, 1, 3), (0, 3, 1, 2))
        needs = (
            ((), (1,), (3, 2), ()),
            ((), (3,), (0,), ()),
            ((), (0,), (), (3,)),
            ((0,), (2,), (1,), ()),
        )
        flow = ((1, 3, 2), (0, 2, 3), (1, 3, 0), (2, 0, 1))

        def pick(table, k):
            spot = table[0][k]
            for i in range(1, n):
                spot = jnp.where(t == i, table[i][k], spot)
            return spot

        pass_on(pick(flow, 0))
        pl.when(relaying)(lambda: pass_on(pick(flow, 1)))

        @pl.when(relaying)
        def _():
            for f in range(cuts):
                block_copy(relay_source, f, relay_source, block_send.at[relay_source, f]).wait_recv()
                relay_copy(f).start()
            line_relay_copy().start()

        def step(k, carry):
            for i in range(n):
                for kk in range(n):
                    for c in needs[i][kk]:
                        pl.when((t == i) & (k == kk))(functools.partial(arrived, c))
            spot = pick(order, 0)
            for kk in range(1, n):
                spot = jnp.where(k == kk, pick(order, kk), spot)
            one(spot)
            return carry

        lax.fori_loop(0, n, step, 0)
        pl.when(relaying)(lambda: pass_on(pick(flow, 2)))
        pl.when(jnp.logical_not(relaying))(lambda: pass_on(pick(flow, 1)))
    else:

        def hold(d, carry):
            arrived((t + d) % n)
            return carry

        lax.fori_loop(1, n, hold, 0)

        def step(d, carry):
            one((t + d) % n)
            return carry

        lax.fori_loop(1, n + 1, step, 0)

    def came(k, carry):
        q = (t + k) % n
        pl.when(k > 0)(lambda: slab_copy(q, q).wait_recv())
        for side in range(2):
            fed(side, lambda: edge_copy(side, q, q).wait_recv())
        return carry

    lax.fori_loop(0, n, came, 0)
    hidden = unfold([slab_in[q].astype(jnp.float32) for q in range(n)])
    top, low = [
        unfold([edge_in[side, q].astype(jnp.float32) for q in range(n)]).reshape(
            frames, 1, cols, width
        )
        for side in range(2)
    ]
    hidden = hidden.reshape(frames, rows, cols, width)
    if rows > 1:
        hidden = jnp.concatenate(
            [hidden[:, :1] + top, hidden[:, 1 : rows - 1], hidden[:, rows - 1 :] + low], axis=1
        )
    else:
        hidden = hidden + top + low
    hidden = hidden.reshape(cells, width) + biases[0:1]
    inner[2:, 1 : rows + 1] = norm_silu(hidden, gains[1:2]).astype(jnp.bfloat16).reshape(
        frames, rows, cols, width
    )
    halo_copies(start)
    if relays:
        pl.when(jnp.logical_not(relaying))(lambda: pass_on(pick(flow, 2)))
    else:

        def passed(d, carry):
            pass_on((t + d) % n)
            return carry

        lax.fori_loop(1, n, passed, 0)
    if shared:

        def crossed(k, carry):
            if relays:
                q = pick(flow, 0)
                for kk in range(1, n - 1):
                    q = jnp.where(k == kk, pick(flow, kk), q)
            else:
                q = (t + 1 + k) % n
            cross(q)
            return carry

        lax.fori_loop(0, n - 1, crossed, 0)
    others(lambda copy: copy.wait())
    halo_came()
    if shared:

        def joined(k, carry):
            q = (t + 1 + k) % n
            for col in range(columns):
                for d in range(1, nc):
                    core_copy(q, col, (core + d) % nc, d).wait_recv()
            return carry

        lax.fori_loop(0, n - 1, joined, 0)
    sums = []
    for e in range(3):
        total = None
        for a in range(3):
            for r in range(3):
                block = inner[a : a + frames, r : r + rows].reshape(cells, width)
                term = lax.dot_general(
                    block, kernel_of(9 * a + 3 * r + e),
                    (((1,), (1,)), ((), ())), preferred_element_type=jnp.float32,
                )
                total = term if total is None else total + term
        sums.append(total)
    hidden = beside(*sums) + biases[1:2]
    merged = feat[...].reshape(cells, width).astype(jnp.float32) + hidden
    active = norm_silu(merged, gains[2:3]).astype(jnp.bfloat16)
    rest = jnp.zeros((LANES - 4 * width_latent, width), jnp.bfloat16)
    latent_wide = jnp.concatenate([latent_rows[...]] * 4 + [rest], axis=0)
    latent = lax.dot_general(
        active, latent_wide, (((1,), (1,)), ((), ())), preferred_element_type=jnp.float32
    )
    cell = lax.broadcasted_iota(jnp.int32, (cells, LANES), 0)
    lane = lax.broadcasted_iota(jnp.int32, (cells, LANES), 1)
    corner = (cell // cols % 2) * 2 + cell % 2
    alive = (t * frames + cell // (rows * cols) < count[0]) & (corner == 0)
    flagged = jnp.where((lane == 4 * width_latent) & alive, 1.0, 0.0)
    patches = jnp.where(lane // width_latent == corner, latent, flagged).astype(jnp.bfloat16)
    spot = lax.broadcasted_iota(jnp.int32, (toks, cells), 1)
    patch = (spot // (2 * cols)) * (cols // 2) + spot % cols // 2
    mine = patch == lax.broadcasted_iota(jnp.int32, (toks, cells), 0)
    patches = jnp.dot(
        jnp.where(mine, 1.0, 0.0).astype(jnp.bfloat16), patches, preferred_element_type=jnp.float32
    ).astype(jnp.bfloat16)
    outgoing = jnp.dot(
        placing[...], patches, preferred_element_type=jnp.float32
    ).astype(jnp.bfloat16)
    tok_out[...] = outgoing.reshape(owners, SUBLANES, LANES)
    tok_in[pl.ds(me, 1)] = tok_out[pl.ds(me, 1)]

    def tok_copy(source, target):
        return pltpu.make_async_remote_copy(
            src_ref=tok_out.at[target], dst_ref=tok_in.at[source],
            send_sem=tok_send.at[target], recv_sem=tok_recv.at[source],
            device_id={"tm": target // ns, "space": target % ns}, device_id_type=MESH,
        )

    def tok_start(d, carry):
        tok_copy(me, (me + d) % owners).start()
        return carry

    def tok_wait(d, carry):
        o = (me + d) % owners
        tok_copy(o, o).wait_recv()
        return carry

    def tok_sent(d, carry):
        tok_copy(me, (me + d) % owners).wait_send()
        return carry

    lax.fori_loop(1, owners, tok_start, 0)
    blocks(lambda copy: copy.wait_send())
    along(None, line_of(lambda copy: copy.wait_send())) if small else around(
        line_of(lambda copy: copy.wait_send())
    )
    if relays:

        @pl.when(relaying)
        def _():
            for f in range(cuts):
                relay_copy(f).wait_send()
            line_relay_copy().wait_send()

    def sent(c, carry):
        pl.when(c != t)(lambda: slab_copy(t, c).wait_send())
        for side in range(2):
            sided(side, lambda: edge_copy(side, t, c).wait_send())
        if shared:

            @pl.when(c != t)
            def _():
                for d in range(1, columns):
                    plane_copy(c, column_of, d).wait_send()
                for col in range(columns):
                    for d in range(1, nc):
                        core_copy(c, col, part_of, d).wait_send()

        return carry

    lax.fori_loop(0, n, sent, 0)
    halo_copies(lambda copy: copy.wait_send())
    lax.fori_loop(1, owners, tok_wait, 0)
    row = lax.broadcasted_iota(jnp.int32, (owners * most, owners * SUBLANES), 0)
    held = lax.broadcasted_iota(jnp.int32, (owners * most, owners * SUBLANES), 1)
    inner = held % SUBLANES
    chosen = (row == held // SUBLANES * most + inner) & (inner < most)
    tokens_out[...] = jnp.dot(
        jnp.where(chosen, 1.0, 0.0).astype(jnp.bfloat16),
        tok_in[...].reshape(owners * SUBLANES, LANES),
        preferred_element_type=jnp.float32,
    ).astype(jnp.bfloat16)
    lax.fori_loop(1, owners, tok_sent, 0)


def embedder(channels, tokens, weight, bias, packed):
    held = tokens[...]
    projected = jnp.dot(held[:, :channels], weight[...], preferred_element_type=jnp.float32)
    flags = held[:, channels : channels + 1].astype(jnp.float32)
    packed[...] = ((projected + bias[...]) * flags).astype(jnp.bfloat16)


def shards(
    features,
    frame_counts,
    routes,
    norm_gains,
    conv_weights,
    conv_biases,
    latent_weight,
    embed_weight,
    embed_bias,
):
    feat = features[0]
    frames, rows, cols, width = feat.shape
    cells = frames * rows * cols
    n, ns = lax.axis_size("tm"), lax.axis_size("space")
    ng, nc = lax.axis_size("groups"), lax.axis_size("clip")
    owners = n * ns
    out = conv_weights.shape[1]
    pack = max(1, LANES // out)
    latents = latent_weight.shape[1]
    tok_count = routes.shape[1]
    most = (tok_count + owners - 1) // owners + 1
    vmem = pl.BlockSpec(memory_space=pltpu.VMEM)
    anywhere = pl.BlockSpec(memory_space=pl.ANY)
    dma = pltpu.SemaphoreType.DMA
    field = pltpu.VMEM((n * frames + 2, rows, cols, width), jnp.bfloat16)
    inner = pltpu.VMEM((frames + 2, rows + 2, cols, width), jnp.bfloat16)
    slab = pltpu.VMEM((n, cells // pack, pack * out), jnp.bfloat16)
    edge = pltpu.VMEM((2, n, frames * cols // pack, pack * out), jnp.bfloat16)
    columns, parts = ng * ns, nc
    if out % (SUBLANES * columns) or width % (LANES * parts):
        columns = parts = 1
    taps = conv_weights.shape[2]
    shares = pltpu.VMEM((n, columns, parts, taps, out // columns, width // parts), jnp.bfloat16)
    cuts = CUTS if frames % CUTS == 0 else 1
    tok = pltpu.VMEM((owners, SUBLANES, LANES), jnp.bfloat16)
    tokens = pl.pallas_call(
        functools.partial(encoder, n, ns, ng, nc, most, latents),
        out_shape=jax.ShapeDtypeStruct((owners * most, LANES), jnp.bfloat16),
        in_specs=[vmem, anywhere, anywhere, vmem, vmem, vmem, vmem,
                  pl.BlockSpec(memory_space=pltpu.SMEM)],
        out_specs=vmem,
        scratch_shapes=[
            field, inner,
            pltpu.VMEM((9, 3 * out, width), jnp.bfloat16),
            shares,
            pltpu.VMEM((owners * SUBLANES, tok_count), jnp.bfloat16),
            slab, slab, edge, edge, tok, tok,
            dma, dma((columns, parts)),
            dma((n, cuts)), dma((cuts,)), dma((n, cuts)),
            dma((n,)), dma((n,)), dma((2, n)), dma((2, n)), dma((5,)), dma((5,)),
            dma((n,)), dma, dma((n,)),
            dma((n, columns)), dma((n, columns)), dma((n, columns, nc)), dma((n, columns, nc)),
            dma((owners,)), dma((owners,)),
        ],
        compiler_params=pltpu.CompilerParams(collective_id=0, has_side_effects=True),
    )(
        feat,
        conv_weights.transpose(0, 2, 1, 3).reshape(2, 9, 3 * out, width),
        conv_weights.transpose(0, 2, 1, 3),
        norm_gains,
        conv_biases,
        latent_weight.T,
        routes.reshape(1, tok_count),
        frame_counts,
    )
    channels = 4 * latents
    embed = embed_weight.shape[1]
    chunk = embed // 1 if embed % (1 * LANES) == 0 else embed
    packed = pl.pallas_call(
        functools.partial(embedder, channels),
        grid=(embed // chunk,),
        out_shape=jax.ShapeDtypeStruct((owners * most, embed), jnp.bfloat16),
        in_specs=[
            pl.BlockSpec((owners * most, LANES), lambda i: (0, 0)),
            pl.BlockSpec((channels, chunk), lambda i: (0, i)),
            pl.BlockSpec((1, chunk), lambda i: (0, i)),
        ],
        out_specs=pl.BlockSpec((owners * most, chunk), lambda i: (0, i)),
    )(tokens, embed_weight, embed_bias.reshape(1, embed))
    return packed[None]


def solution(mesh):
    return jax.shard_map(
        shards,
        mesh=mesh,
        in_specs=(
            P(("groups", "clip"), "tm", "space", None, None),
            P(("groups", "clip")),
            P(("groups", "clip"), ("tm", "space"), None),
            P(),
            P(None, "tm", None, None),
            P(),
            P(),
            P(),
            P(),
        ),
        out_specs=P(("groups", "clip"), ("tm", "space"), None),
        check_vma=False,
    )
```

time: 52.2 us -> 48.9 us (0.937)
  Pallas kernels: 51.4 us -> 47.9 us
    pallas_call x1, Pallas kernels: 49.4 us -> 45.9 us  [shards(): pl.pallas_call(functools.partial(encoder, n, ns, ng, nc, most, latents),...]
where the time goes in v2:
time: 48.9 us; the launch traced here: 48.5 us
  Pallas kernels  47.9 us (98%)
  between operations  0.66 us (1%)
    pallas_call x1, Pallas kernels, shards(): pl.pallas_call(functools.partial(encoder, n, ns, ng, nc, most, latents),...  45.9 us
    pallas_call x1, Pallas kernels, shards(): pl.pallas_call(functools.partial(embedder, channels), grid=(embed // chun...  2.02 us

profile of v2, /device:TPU:0, one launch (start us, length us, event | category | flops | bytes accessed | tf_op | source)
XLA Modules:
  0.0 48.5 jit_solution(8017359562067299131)
XLA Ops:
  0.7 45.9 %shard_map.91.tokens = bf16[72,128]{1,0:T(8,128)(2,1)} custom-call(bf16[4,4,16,256]{3,2,1,0:T(8,128)(2,1)} %bitcast.10, bf16[2,9,192,256]{3,2,1,0:T(8,128)(2,1)} %bitcast.8, bf16[2,27,64,256]{3,2,1,0:T(8,128)(2,1)} %bitcast.9, f32[3,256]{1,0:T(4,128)} %gains.1, f32[2,256]{1,0:T(2,128)} %biases.1, bf16[16,256]{1,0:T(8,128)(2,1)} %bitcast.12, ...), custom_call_target="tpu_custom_call" | custom-call | tf_op jit(solution)/shard_map/pallas_call | solution.py:625
  46.5 2.0 %shard_map.92 = bf16[72,3072]{1,0:T(8,128)(2,1)} custom-call(bf16[72,128]{1,0:T(8,128)(2,1)} %shard_map.91.tokens, bf16[64,3072]{1,0:T(8,128)(2,1)} %weight.1, f32[1,3072]{1,0:T(1,128)} %bitcast.11), custom_call_target="tpu_custom_call" | custom-call | tf_op jit(solution)/shard_map/pallas_call | solution.py:658

commit v3 on v2

--- a/solution.py
+++ b/solution.py
@@ -11,6 +11,7 @@
 LANES = 128
 SUBLANES = 16
 CUTS = 4
+GRANT = 28 << 20
 
 
 def norm_silu(values, gain):
@@ -21,12 +22,12 @@
 
 def encoder(
     n, ns, ng, nc, most, width_latent,
-    feat, weights_any, shares_any, gains, biases, latent_rows, owner_of, count,
+    feat_any, weights_any, shares_any, gains_any, biases_any, latent_any, owner_any, count,
     tokens_out,
-    field, inner, taps, shares, placing, slab_out, slab_in, edge_out, edge_in, tok_out, tok_in,
-    raw_sem, share_sem, block_send, relay_send, block_recv,
+    feat, gains, biases, latent_rows, owner_of, field, inner, taps, shares, placing, slab_out, slab_in, edge_out, edge_in, tok_out, tok_in,
+    load_sem, raw_sem, share_sem, block_send, relay_send, block_recv,
     slab_send, slab_recv, edge_send, edge_recv, halo_send, halo_recv,
-    line_send, line_relay, line_recv, plane_send, plane_recv, core_send, core_recv,
+    line_send, line_relay_send, line_recv, plane_send, plane_recv, core_send, core_recv,
     tok_send, tok_recv,
 ):
     t = lax.axis_index("tm")
@@ -80,7 +81,18 @@
             shares.at[t, col, part], share_sem.at[col, part],
         )
 
+    loads = [
+        pltpu.make_async_copy(source, target, load_sem.at[i])
+        for i, (source, target) in enumerate((
+            (feat_any, feat), (gains_any, gains), (owner_any, owner_of),
+            (biases_any, biases), (latent_any, latent_rows),
+        ))
+    ]
+    for copy in loads[:2]:
+        copy.start()
     share_load(column_of, part_of).start()
+    for copy in loads[2:]:
+        copy.start()
     weight_copy.start()
 
     def others(act):
@@ -106,6 +118,8 @@
         edge_in[1] = jnp.zeros(edge_in.shape[1:], edge_in.dtype)
         inner[:, rows + 1 :] = jnp.zeros((inner.shape[0], 1) + inner.shape[2:], inner.dtype)
 
+    for copy in loads[:2]:
+        copy.wait()
     inputs = feat[...].reshape(cells, width).astype(jnp.float32)
 
     def block_copy(c, f, target, send_sem):
@@ -159,15 +173,9 @@
             device_id={"clip": (core + d) % nc}, device_id_type=MESH,
         )
 
-    def along(first, act):
-        for d in range(n - 1, 0, -1):
-            if first is not None and (d == 1) != first:
-                continue
-            for target in (t - d, t + d):
-                here = (target >= 0) & (target < n)
-                if relays and d == 2:
-                    here = here & ((t == 0) | (t == n - 1))
-                pl.when(here)(functools.partial(act, (target + n) % n))
+    def beside_line(act):
+        for target in (t - 1, t + 1):
+            pl.when((target >= 0) & (target < n))(functools.partial(act, (target + n) % n))
 
     def around(act):
         def each(d, carry):
@@ -176,27 +184,36 @@
 
         lax.fori_loop(1, n, each, 0)
 
-    small = n <= 8
-
+    reach = beside_line if relays else around
     def blocks(act):
         def each(spot):
             for f in range(cuts):
                 act(block_copy(t, f, spot, block_send.at[spot, f]))
 
-        along(None, each) if small else around(each)
+        reach(each)
 
     def line_of(act):
         return lambda spot: act(line_copy(t, spot, line_send.at[spot]))
 
-    relay_target = jnp.where(t == 1, 0, n - 1)
-    relay_source = jnp.where(t == 1, 2, 1)
-    relaying = (t == 1) | (t == 2)
-
-    def relay_copy(f):
-        return block_copy(relay_source, f, relay_target, relay_send.at[f])
-
-    def line_relay_copy():
-        return line_copy(relay_source, relay_target, line_relay)
+    middle = (t == 1) | (t == 2)
+    low = t == 1
+    end, mate, far = [jnp.where(low, one, two) for one, two in ((0, 3), (2, 1), (3, 0))]
+    courses = ((end, mate), (mate, end), (far, end))
+
+    def relay_copy(i, f):
+        q, target = courses[i]
+        return block_copy(q, f, target, relay_send.at[i, f])
+
+    def line_relay(i):
+        q, target = courses[i]
+        return line_copy(q, target, line_relay_send.at[i])
+
+    def relay_block(*which):
+        for f in range(cuts):
+            for i in which:
+                q = courses[i][0]
+                block_copy(q, f, q, block_send.at[q, f]).wait_recv()
+                relay_copy(i, f).start()
 
     def pass_on(q):
         line_copy(q, q, line_send.at[q]).wait_recv()
@@ -342,6 +359,8 @@
     field[pl.ds(2 + frames * t, frames)] = norm_silu(inputs, gains[0:1]).astype(
         jnp.bfloat16
     ).reshape(frames, rows, cols, width)
+    for copy in loads[2:]:
+        copy.wait()
     toks = owner_of.shape[1]
     before = lax.broadcasted_iota(jnp.int32, (toks, toks), 0)
     after = lax.broadcasted_iota(jnp.int32, (toks, toks), 1)
@@ -354,23 +373,31 @@
     share_load(column_of, part_of).wait()
     pl.semaphore_wait(barrier, expected)
     start = lambda copy: copy.start()
-    if small:
-        along(True, line_of(start))
-        blocks(start)
-        along(False, line_of(start))
-    else:
-        blocks(start)
-        around(line_of(start))
+    reach(line_of(start))
+    blocks(start)
     weight_copy.wait()
     if relays:
-        order = ((0, 1, 3, 2), (2, 3, 0, 1), (2, 0, 1, 3), (0, 3, 1, 2))
-        needs = (
-            ((), (1,), (3, 2), ()),
-            ((), (3,), (0,), ()),
-            ((), (0,), (), (3,)),
-            ((0,), (2,), (1,), ()),
-        )
-        flow = ((1, 3, 2), (0, 2, 3), (1, 3, 0), (2, 0, 1))
+        order = ((0, 1, 2, 3), (3, 2, 0, 1), (0, 3, 1, 2), (3, 2, 0, 1))
+        flow = ((1, 2, 3), (0, 2, 3), (3, 1, 0), (2, 1, 0))
+
+        def forward():
+            pass_on(end)
+            pass_on(mate)
+            relay_block(0, 1)
+            line_relay(0).start()
+            line_relay(1).start()
+            relay_block(2)
+
+        def last(q):
+            pass_on(q)
+            line_relay(2).start()
+
+        before = (
+            ((), ((pass_on, 1), (arrived, 1)), ((arrived, 2),), ((pass_on, 2), (arrived, 3))),
+            ((), (), ((last, 3),), ()),
+            ((), (), ((last, 0),), ()),
+            (((pass_on, 2), (arrived, 2)), ((arrived, 1),), ((pass_on, 1), (arrived, 0)), ()),
+        )
 
         def pick(table, k):
             spot = table[0][k]
@@ -378,30 +405,29 @@
                 spot = jnp.where(t == i, table[i][k], spot)
             return spot
 
-        pass_on(pick(flow, 0))
-        pl.when(relaying)(lambda: pass_on(pick(flow, 1)))
-
-        @pl.when(relaying)
-        def _():
-            for f in range(cuts):
-                block_copy(relay_source, f, relay_source, block_send.at[relay_source, f]).wait_recv()
-                relay_copy(f).start()
-            line_relay_copy().start()
+        def chosen(table, k):
+            spot = pick(table, 0)
+            for kk in range(1, len(table[0])):
+                spot = jnp.where(k == kk, pick(table, kk), spot)
+            return spot
+
+        pl.when(middle)(forward)
 
         def step(k, carry):
             for i in range(n):
                 for kk in range(n):
-                    for c in needs[i][kk]:
-                        pl.when((t == i) & (k == kk))(functools.partial(arrived, c))
-            spot = pick(order, 0)
-            for kk in range(1, n):
-                spot = jnp.where(k == kk, pick(order, kk), spot)
-            one(spot)
+                    if before[i][kk]:
+
+                        @pl.when((t == i) & (k == kk))
+                        def _():
+                            for act, c in before[i][kk]:
+                                act(c)
+
+            one(chosen(order, k))
             return carry
 
         lax.fori_loop(0, n, step, 0)
-        pl.when(relaying)(lambda: pass_on(pick(flow, 2)))
-        pl.when(jnp.logical_not(relaying))(lambda: pass_on(pick(flow, 1)))
+        pl.when(jnp.logical_not(middle))(lambda: pass_on(pick(flow, 2)))
     else:
 
         def hold(d, carry):
@@ -425,7 +451,7 @@
 
     lax.fori_loop(0, n, came, 0)
     hidden = unfold([slab_in[q].astype(jnp.float32) for q in range(n)])
-    top, low = [
+    top, bottom = [
         unfold([edge_in[side, q].astype(jnp.float32) for q in range(n)]).reshape(
             frames, 1, cols, width
         )
@@ -434,18 +460,16 @@
     hidden = hidden.reshape(frames, rows, cols, width)
     if rows > 1:
         hidden = jnp.concatenate(
-            [hidden[:, :1] + top, hidden[:, 1 : rows - 1], hidden[:, rows - 1 :] + low], axis=1
+            [hidden[:, :1] + top, hidden[:, 1 : rows - 1], hidden[:, rows - 1 :] + bottom], axis=1
         )
     else:
-        hidden = hidden + top + low
+        hidden = hidden + top + bottom
     hidden = hidden.reshape(cells, width) + biases[0:1]
     inner[2:, 1 : rows + 1] = norm_silu(hidden, gains[1:2]).astype(jnp.bfloat16).reshape(
         frames, rows, cols, width
     )
     halo_copies(start)
-    if relays:
-        pl.when(jnp.logical_not(relaying))(lambda: pass_on(pick(flow, 2)))
-    else:
+    if not relays:
 
         def passed(d, carry):
             pass_on((t + d) % n)
@@ -456,9 +480,7 @@
 
         def crossed(k, carry):
             if relays:
-                q = pick(flow, 0)
-                for kk in range(1, n - 1):
-                    q = jnp.where(k == kk, pick(flow, kk), q)
+                q = chosen(flow, k)
             else:
                 q = (t + 1 + k) % n
             cross(q)
@@ -537,16 +559,15 @@
 
     lax.fori_loop(1, owners, tok_start, 0)
     blocks(lambda copy: copy.wait_send())
-    along(None, line_of(lambda copy: copy.wait_send())) if small else around(
-        line_of(lambda copy: copy.wait_send())
-    )
+    reach(line_of(lambda copy: copy.wait_send()))
     if relays:
 
-        @pl.when(relaying)
+        @pl.when(middle)
         def _():
-            for f in range(cuts):
-                relay_copy(f).wait_send()
-            line_relay_copy().wait_send()
+            for i in range(3):
+                for f in range(cuts):
+                    relay_copy(i, f).wait_send()
+                line_relay(i).wait_send()
 
     def sent(c, carry):
         pl.when(c != t)(lambda: slab_copy(t, c).wait_send())
@@ -609,7 +630,8 @@
     tok_count = routes.shape[1]
     most = (tok_count + owners - 1) // owners + 1
     vmem = pl.BlockSpec(memory_space=pltpu.VMEM)
-    anywhere = pl.BlockSpec(memory_space=pl.ANY)
+    hbm = pl.BlockSpec(memory_space=pltpu.HBM)
+    away = lambda value: pltpu.with_memory_space_constraint(value, pltpu.HBM)
     dma = pltpu.SemaphoreType.DMA
     field = pltpu.VMEM((n * frames + 2, rows, cols, width), jnp.bfloat16)
     inner = pltpu.VMEM((frames + 2, rows + 2, cols, width), jnp.bfloat16)
@@ -625,31 +647,37 @@
     tokens = pl.pallas_call(
         functools.partial(encoder, n, ns, ng, nc, most, latents),
         out_shape=jax.ShapeDtypeStruct((owners * most, LANES), jnp.bfloat16),
-        in_specs=[vmem, anywhere, anywhere, vmem, vmem, vmem, vmem,
-                  pl.BlockSpec(memory_space=pltpu.SMEM)],
+        in_specs=[hbm] * 7 + [pl.BlockSpec(memory_space=pltpu.SMEM)],
         out_specs=vmem,
         scratch_shapes=[
+            pltpu.VMEM(feat.shape, feat.dtype),
+            pltpu.VMEM(norm_gains.shape, norm_gains.dtype),
+            pltpu.VMEM(conv_biases.shape, conv_biases.dtype),
+            pltpu.VMEM((latents, width), latent_weight.dtype),
+            pltpu.VMEM((1, tok_count), routes.dtype),
             field, inner,
             pltpu.VMEM((9, 3 * out, width), jnp.bfloat16),
             shares,
             pltpu.VMEM((owners * SUBLANES, tok_count), jnp.bfloat16),
             slab, slab, edge, edge, tok, tok,
-            dma, dma((columns, parts)),
-            dma((n, cuts)), dma((cuts,)), dma((n, cuts)),
+            dma((5,)), dma, dma((columns, parts)),
+            dma((n, cuts)), dma((3, cuts)), dma((n, cuts)),
             dma((n,)), dma((n,)), dma((2, n)), dma((2, n)), dma((5,)), dma((5,)),
-            dma((n,)), dma, dma((n,)),
+            dma((n,)), dma((3,)), dma((n,)),
             dma((n, columns)), dma((n, columns)), dma((n, columns, nc)), dma((n, columns, nc)),
             dma((owners,)), dma((owners,)),
         ],
-        compiler_params=pltpu.CompilerParams(collective_id=0, has_side_effects=True),
+        compiler_params=pltpu.CompilerParams(
+            collective_id=0, has_side_effects=True, vmem_limit_bytes=GRANT
+        ),
     )(
-        feat,
-        conv_weights.transpose(0, 2, 1, 3).reshape(2, 9, 3 * out, width),
-        conv_weights.transpose(0, 2, 1, 3),
-        norm_gains,
-        conv_biases,
-        latent_weight.T,
-        routes.reshape(1, tok_count),
+        away(feat),
+        away(conv_weights.transpose(0, 2, 1, 3).reshape(2, 9, 3 * out, width)),
+        away(conv_weights.transpose(0, 2, 1, 3)),
+        away(norm_gains),
+        away(conv_biases),
+        away(latent_weight.T),
+        away(routes.reshape(1, tok_count)),
         frame_counts,
     )
     channels = 4 * latents
@@ -665,6 +693,7 @@
             pl.BlockSpec((1, chunk), lambda i: (0, i)),
         ],
         out_specs=pl.BlockSpec((owners * most, chunk), lambda i: (0, i)),
+        compiler_params=pltpu.CompilerParams(vmem_limit_bytes=GRANT),
     )(tokens, embed_weight, embed_bias.reshape(1, embed))
     return packed[None]
 

time: 48.9 us -> 41.4 us (0.85)
  Pallas kernels: 47.9 us -> 40.5 us
    pallas_call x1, Pallas kernels: 45.9 us -> 39.5 us  [shards(): pl.pallas_call(functools.partial(encoder, n, ns, ng, nc, most, latents),...]
    pallas_call x1, Pallas kernels: 2.02 us -> 1.03 us  [shards(): pl.pallas_call(functools.partial(embedder, channels), grid=(embed // chun...]
where the time goes in v3:
time: 41.4 us; the launch traced here: 41.2 us
  Pallas kernels  40.5 us (98%)
  between operations  0.69 us (2%)
    pallas_call x1, Pallas kernels, shards(): pl.pallas_call(functools.partial(encoder, n, ns, ng, nc, most, latents),...  39.5 us
    pallas_call x1, Pallas kernels, shards(): pl.pallas_call(functools.partial(embedder, channels), grid=(embed // chun...  1.03 us

profile of v3, /device:TPU:0, one launch (start us, length us, event | category | flops | bytes accessed | tf_op | source)
XLA Modules:
  0.0 41.2 jit_solution(7519834664895021272)
XLA Ops:
  0.7 0.0 copy-start
  0.7 0.0 copy-start.1
  0.7 39.5 %shard_map.91.tokens = bf16[72,128]{1,0:T(8,128)(2,1)S(1)} custom-call(bf16[4,4,16,256]{3,2,1,0:T(8,128)(2,1)} %bitcast.11, bf16[2,9,192,256]{3,2,1,0:T(8,128)(2,1)} %bitcast.9, bf16[2,27,64,256]{3,2,1,0:T(8,128)(2,1)} %bitcast.10, f32[3,256]{1,0:T(4,128)} %gains_any.1, f32[2,256]{1,0:T(2,128)} %biases_any.1, bf16[16,256]{1,0:T(8,128)(2,1)} %bitcast.12, ...), custom_call_target="tpu_custom_call" | custom-call | tf_op jit(solution)/shard_map/pallas_call | solution.py:647
  40.2 0.0 copy-done
  40.2 0.0 copy-done.1
  40.2 1.0 %shard_map.92 = bf16[72,3072]{1,0:T(8,128)(2,1)} custom-call(bf16[72,128]{1,0:T(8,128)(2,1)S(1)} %shard_map.91.tokens, bf16[64,3072]{1,0:T(8,128)(2,1)S(1)} %copy-done, f32[1,3072]{1,0:T(1,128)S(1)} %bitcast.8), custom_call_target="tpu_custom_call" | custom-call | tf_op jit(solution)/shard_map/pallas_call | solution.py:686
Async XLA Ops:
  0.7 39.5 %copy-start = (bf16[64,3072]{1,0:T(8,128)(2,1)S(1)}, bf16[64,3072]{1,0:T(8,128)(2,1)}, u32[]{:S(2)}) copy-start(bf16[64,3072]{1,0:T(8,128)(2,1)} %weight.1) | copy-start | bytes 1179652
  0.7 39.5 %copy-start.1 = (f32[3072]{0:T(1024)S(1)}, f32[3072]{0:T(1024)}, u32[]{:S(2)}) copy-start(f32[3072]{0:T(1024)} %param.17) | copy-start | bytes 36868

commit v4 on v3

--- a/solution.py
+++ b/solution.py
@@ -11,6 +11,7 @@
 LANES = 128
 SUBLANES = 16
 CUTS = 4
+BITS = 3
 GRANT = 28 << 20
 
 
@@ -24,11 +25,9 @@
     n, ns, ng, nc, most, width_latent,
     feat_any, weights_any, shares_any, gains_any, biases_any, latent_any, owner_any, count,
     tokens_out,
-    feat, gains, biases, latent_rows, owner_of, field, inner, taps, shares, placing, slab_out, slab_in, edge_out, edge_in, tok_out, tok_in,
-    load_sem, raw_sem, share_sem, block_send, relay_send, block_recv,
-    slab_send, slab_recv, edge_send, edge_recv, halo_send, halo_recv,
-    line_send, line_relay_send, line_recv, plane_send, plane_recv, core_send, core_recv,
-    tok_send, tok_recv,
+    feat, gains, biases, latent_rows, owner_of, field, inner, taps, mine, shares, placing, slab_out, slab_in, edge_out, edge_in, tok_out, tok_in,
+    load_sem, raw_sem, share_sem, block_send, relay_send, block_recv, slab_sem, edge_sem,
+    halo_send, halo_recv, line_send, line_relay_send, line_recv, plane_recv, bulk_sem, tok_sem,
 ):
     t = lax.axis_index("tm")
     s = lax.axis_index("space")
@@ -43,7 +42,9 @@
     size = frames // cuts
     pack = max(1, LANES // out)
     relays = n == 4
-    columns, parts, _, share_rows, share_lanes = shares.shape[1:]
+    columns, parts, share_taps, share_rows, share_lanes = shares.shape[1:]
+    bits = line_recv.shape[1]
+    bit = share_taps // bits
     shared = columns > 1
     column_of = g * ns + s if shared else 0
     part_of = core if shared else 0
@@ -74,13 +75,13 @@
             expected += 1
     weight_copy = pltpu.make_async_copy(weights_any.at[0], taps, raw_sem)
 
-    def share_load(col, part):
+    def share_load(col, part, target, sem):
         lanes = pl.ds(pl.multiple_of(part * share_lanes, LANES), share_lanes)
         return pltpu.make_async_copy(
-            shares_any.at[1, :, pl.ds(col * share_rows, share_rows), lanes],
-            shares.at[t, col, part], share_sem.at[col, part],
-        )
-
+            shares_any.at[1, :, pl.ds(col * share_rows, share_rows), lanes], target, sem
+        )
+
+    mine_load = share_load(column_of, part_of, mine, share_sem.at[0])
     loads = [
         pltpu.make_async_copy(source, target, load_sem.at[i])
         for i, (source, target) in enumerate((
@@ -90,17 +91,14 @@
     ]
     for copy in loads[:2]:
         copy.start()
-    share_load(column_of, part_of).start()
+    mine_load.start()
     for copy in loads[2:]:
         copy.start()
     weight_copy.start()
 
-    def others(act):
-        for col in range(columns):
-            for part in range(parts):
-                pl.when((column_of != col) | (part_of != part))(lambda: act(share_load(col, part)))
-
-    others(lambda copy: copy.start())
+    for col in range(columns):
+        for part in range(parts):
+            share_load(col, part, shares.at[t, col, part], share_sem.at[1]).start()
 
     field[0:2] = jnp.zeros((2,) + field.shape[1:], field.dtype)
 
@@ -132,15 +130,22 @@
     def slab_copy(source, target):
         return pltpu.make_async_remote_copy(
             src_ref=slab_out.at[target], dst_ref=slab_in.at[source],
-            send_sem=slab_send.at[target], recv_sem=slab_recv.at[source],
+            send_sem=slab_sem.at[0], recv_sem=slab_sem.at[1],
             device_id={"tm": target}, device_id_type=MESH,
         )
 
     def edge_copy(side, source, target):
         return pltpu.make_async_remote_copy(
             src_ref=edge_out.at[side, target], dst_ref=edge_in.at[side, source],
-            send_sem=edge_send.at[side, target], recv_sem=edge_recv.at[side, source],
+            send_sem=edge_sem.at[0, side], recv_sem=edge_sem.at[1, side],
             device_id={"tm": target, "space": (s + 1 - 2 * side + ns) % ns}, device_id_type=MESH,
+        )
+
+    def gathered(ref, send_sem, recv_sem=None):
+        return pltpu.make_async_remote_copy(
+            src_ref=ref, dst_ref=ref, send_sem=send_sem,
+            recv_sem=send_sem if recv_sem is None else recv_sem,
+            device_id={"tm": t}, device_id_type=MESH,
         )
 
     def sided(side, act):
@@ -149,51 +154,52 @@
     def fed(side, act):
         pl.when(s > 0 if side == 0 else s < ns - 1)(act)
 
-    def line_copy(q, target, send_sem):
-        piece = shares.at[q, column_of, part_of]
+    def line_copy(q, k, target, send_sem, own=False):
+        piece = shares.at[q, column_of, part_of, pl.ds(bit * k, bit)]
         return pltpu.make_async_remote_copy(
-            src_ref=piece, dst_ref=piece, send_sem=send_sem, recv_sem=line_recv.at[q],
+            src_ref=mine.at[pl.ds(bit * k, bit)] if own else piece, dst_ref=piece,
+            send_sem=send_sem, recv_sem=line_recv.at[q, k],
             device_id={"tm": target}, device_id_type=MESH,
         )
 
-    def plane_copy(q, col, d):
-        piece = shares.at[q, col, part_of]
+    def plane_copy(q, k, d):
+        piece = shares.at[q, column_of, part_of, pl.ds(bit * k, bit)]
         peer = (column_of + d) % columns
         return pltpu.make_async_remote_copy(
-            src_ref=piece, dst_ref=piece,
-            send_sem=plane_send.at[q, d], recv_sem=plane_recv.at[q, col],
+            src_ref=piece, dst_ref=piece, send_sem=bulk_sem.at[0],
+            recv_sem=plane_recv.at[(q - t + n) % n - 1, k],
             device_id={"groups": peer // ns, "space": peer % ns}, device_id_type=MESH,
         )
 
-    def core_copy(q, col, part, d):
-        piece = shares.at[q, col, part]
+    def core_copy(q, col, k, d):
+        piece = shares.at[q, col, part_of, pl.ds(bit * k, bit)]
         return pltpu.make_async_remote_copy(
-            src_ref=piece, dst_ref=piece,
-            send_sem=core_send.at[q, col, d], recv_sem=core_recv.at[q, col, part],
+            src_ref=piece, dst_ref=piece, send_sem=bulk_sem.at[1], recv_sem=bulk_sem.at[2],
             device_id={"clip": (core + d) % nc}, device_id_type=MESH,
         )
 
     def beside_line(act):
-        for target in (t - 1, t + 1):
-            pl.when((target >= 0) & (target < n))(functools.partial(act, (target + n) % n))
+        for way in range(2):
+            target = t - 1 + 2 * way
+            pl.when((target >= 0) & (target < n))(
+                functools.partial(act, (target + n) % n, way)
+            )
 
     def around(act):
         def each(d, carry):
-            act((t + d) % n)
+            act((t + d) % n, 0)
             return carry
 
         lax.fori_loop(1, n, each, 0)
 
     reach = beside_line if relays else around
-    def blocks(act):
-        def each(spot):
-            for f in range(cuts):
-                act(block_copy(t, f, spot, block_send.at[spot, f]))
-
-        reach(each)
-
-    def line_of(act):
-        return lambda spot: act(line_copy(t, spot, line_send.at[spot]))
+    def send_blocks(spot, way):
+        for f in range(cuts):
+            block_copy(t, f, spot, block_send.at[way]).start()
+
+    def send_lines(spot, way):
+        for k in range(bits):
+            line_copy(t, k, spot, line_send.at[way], own=True).start()
 
     middle = (t == 1) | (t == 2)
     low = t == 1
@@ -202,37 +208,47 @@
 
     def relay_copy(i, f):
         q, target = courses[i]
-        return block_copy(q, f, target, relay_send.at[i, f])
-
-    def line_relay(i):
+        return block_copy(q, f, target, relay_send.at[i])
+
+    def line_relay(i, k):
         q, target = courses[i]
-        return line_copy(q, target, line_relay_send.at[i])
+        return line_copy(q, k, target, line_relay_send.at[i])
 
     def relay_block(*which):
         for f in range(cuts):
             for i in which:
                 q = courses[i][0]
-                block_copy(q, f, q, block_send.at[q, f]).wait_recv()
+                block_copy(q, f, q, block_send.at[0]).wait_recv()
                 relay_copy(i, f).start()
 
-    def pass_on(q):
-        line_copy(q, q, line_send.at[q]).wait_recv()
+    def pass_bit(q, k):
         if shared:
             for d in range(1, columns):
-                plane_copy(q, column_of, d).start()
+                plane_copy(q, k, d).start()
             for d in range(1, nc):
-                core_copy(q, column_of, part_of, d).start()
+                core_copy(q, column_of, k, d).start()
+
+    def line_came(q, k):
+        line_copy(q, k, q, line_send.at[0]).wait_recv()
+
+    def pass_on(q):
+        for k in range(bits):
+            line_came(q, k)
+            pass_bit(q, k)
 
     def cross(q):
-        for d in range(1, columns):
-            col = (column_of + d) % columns
-            plane_copy(q, col, d).wait_recv()
-            for dc in range(1, nc):
-                core_copy(q, col, part_of, dc).start()
+        for k in range(bits):
+            gathered(
+                shares.at[0, pl.ds(0, columns - 1), 0, pl.ds(0, bit)],
+                bulk_sem.at[0], plane_recv.at[(q - t + n) % n - 1, k],
+            ).wait_recv()
+            for d in range(1, columns):
+                for dc in range(1, nc):
+                    core_copy(q, (column_of + d) % columns, k, dc).start()
 
     def arrived(c):
         for f in range(cuts):
-            block_copy(c, f, c, block_send.at[c, f]).wait_recv()
+            block_copy(c, f, c, block_send.at[0]).wait_recv()
 
     grid_rows = rows + 2
     column = lax.broadcasted_iota(jnp.int32, (frames * grid_rows * cols, 1), 0) % cols
@@ -370,11 +386,11 @@
     rank = jnp.sum(jnp.where(same, 1, 0), axis=0, keepdims=True)
     slots = lax.broadcasted_iota(jnp.int32, (owners * SUBLANES, toks), 0)
     placing[...] = jnp.where(slots == owner * SUBLANES + rank, 1.0, 0.0).astype(jnp.bfloat16)
-    share_load(column_of, part_of).wait()
+    mine_load.wait()
     pl.semaphore_wait(barrier, expected)
     start = lambda copy: copy.start()
-    reach(line_of(start))
-    blocks(start)
+    reach(send_lines)
+    reach(send_blocks)
     weight_copy.wait()
     if relays:
         order = ((0, 1, 2, 3), (3, 2, 0, 1), (0, 3, 1, 2), (3, 2, 0, 1))
@@ -384,13 +400,16 @@
             pass_on(end)
             pass_on(mate)
             relay_block(0, 1)
-            line_relay(0).start()
-            line_relay(1).start()
+            for k in range(bits):
+                line_relay(0, k).start()
+                line_relay(1, k).start()
             relay_block(2)
 
         def last(q):
-            pass_on(q)
-            line_relay(2).start()
+            for k in range(bits):
+                line_came(q, k)
+                line_relay(2, k).start()
+                pass_bit(q, k)
 
         before = (
             ((), ((pass_on, 1), (arrived, 1)), ((arrived, 2),), ((pass_on, 2), (arrived, 3))),
@@ -442,14 +461,9 @@
 
         lax.fori_loop(1, n + 1, step, 0)
 
-    def came(k, carry):
-        q = (t + k) % n
-        pl.when(k > 0)(lambda: slab_copy(q, q).wait_recv())
-        for side in range(2):
-            fed(side, lambda: edge_copy(side, q, q).wait_recv())
-        return carry
-
-    lax.fori_loop(0, n, came, 0)
+    gathered(slab_in.at[pl.ds(0, n - 1)], slab_sem.at[0], slab_sem.at[1]).wait_recv()
+    for side in range(2):
+        fed(side, lambda: gathered(edge_in.at[side], edge_sem.at[0, side], edge_sem.at[1, side]).wait_recv())
     hidden = unfold([slab_in[q].astype(jnp.float32) for q in range(n)])
     top, bottom = [
         unfold([edge_in[side, q].astype(jnp.float32) for q in range(n)]).reshape(
@@ -487,18 +501,11 @@
             return carry
 
         lax.fori_loop(0, n - 1, crossed, 0)
-    others(lambda copy: copy.wait())
+    pltpu.make_async_copy(shares.at[t], shares.at[t], share_sem.at[1]).wait()
     halo_came()
     if shared:
 
-        def joined(k, carry):
-            q = (t + 1 + k) % n
-            for col in range(columns):
-                for d in range(1, nc):
-                    core_copy(q, col, (core + d) % nc, d).wait_recv()
-            return carry
-
-        lax.fori_loop(0, n - 1, joined, 0)
+        gathered(shares.at[pl.ds(0, n - 1), :, 0], bulk_sem.at[1], bulk_sem.at[2]).wait_recv()
     sums = []
     for e in range(3):
         total = None
@@ -537,57 +544,41 @@
     tok_out[...] = outgoing.reshape(owners, SUBLANES, LANES)
     tok_in[pl.ds(me, 1)] = tok_out[pl.ds(me, 1)]
 
-    def tok_copy(source, target):
-        return pltpu.make_async_remote_copy(
-            src_ref=tok_out.at[target], dst_ref=tok_in.at[source],
-            send_sem=tok_send.at[target], recv_sem=tok_recv.at[source],
+    def tok_start(d, carry):
+        target = (me + d) % owners
+        pltpu.make_async_remote_copy(
+            src_ref=tok_out.at[target], dst_ref=tok_in.at[me],
+            send_sem=tok_sem.at[0], recv_sem=tok_sem.at[1],
             device_id={"tm": target // ns, "space": target % ns}, device_id_type=MESH,
-        )
-
-    def tok_start(d, carry):
-        tok_copy(me, (me + d) % owners).start()
+        ).start()
         return carry
 
-    def tok_wait(d, carry):
-        o = (me + d) % owners
-        tok_copy(o, o).wait_recv()
-        return carry
-
-    def tok_sent(d, carry):
-        tok_copy(me, (me + d) % owners).wait_send()
-        return carry
-
     lax.fori_loop(1, owners, tok_start, 0)
-    blocks(lambda copy: copy.wait_send())
-    reach(line_of(lambda copy: copy.wait_send()))
+    def line_sent(_, way):
+        count = 1 if relays else n - 1
+        gathered(field.at[pl.ds(0, frames * count)], block_send.at[way]).wait_send()
+        gathered(shares.at[pl.ds(0, count), 0, 0], line_send.at[way]).wait_send()
+
     if relays:
+        beside_line(line_sent)
 
         @pl.when(middle)
         def _():
             for i in range(3):
-                for f in range(cuts):
-                    relay_copy(i, f).wait_send()
-                line_relay(i).wait_send()
-
-    def sent(c, carry):
-        pl.when(c != t)(lambda: slab_copy(t, c).wait_send())
-        for side in range(2):
-            sided(side, lambda: edge_copy(side, t, c).wait_send())
-        if shared:
-
-            @pl.when(c != t)
-            def _():
-                for d in range(1, columns):
-                    plane_copy(c, column_of, d).wait_send()
-                for col in range(columns):
-                    for d in range(1, nc):
-                        core_copy(c, col, part_of, d).wait_send()
-
-        return carry
-
-    lax.fori_loop(0, n, sent, 0)
+                gathered(field.at[pl.ds(0, frames)], relay_send.at[i]).wait_send()
+                gathered(shares.at[0, 0, 0], line_relay_send.at[i]).wait_send()
+
+    else:
+        line_sent(0, 0)
+    gathered(slab_out.at[pl.ds(0, n - 1)], slab_sem.at[0]).wait_send()
+    for side in range(2):
+        sided(side, lambda: gathered(edge_out.at[side], edge_sem.at[0, side]).wait_send())
+    if shared:
+        gathered(shares.at[pl.ds(0, n - 1), pl.ds(0, columns - 1), 0], bulk_sem.at[0]).wait_send()
+        gathered(shares.at[pl.ds(0, n - 1), :, 0], bulk_sem.at[1]).wait_send()
     halo_copies(lambda copy: copy.wait_send())
-    lax.fori_loop(1, owners, tok_wait, 0)
+    everyone = gathered(tok_in.at[pl.ds(0, owners - 1)], tok_sem.at[0], tok_sem.at[1])
+    everyone.wait_recv()
     row = lax.broadcasted_iota(jnp.int32, (owners * most, owners * SUBLANES), 0)
     held = lax.broadcasted_iota(jnp.int32, (owners * most, owners * SUBLANES), 1)
     inner = held % SUBLANES
@@ -597,7 +588,7 @@
         tok_in[...].reshape(owners * SUBLANES, LANES),
         preferred_element_type=jnp.float32,
     ).astype(jnp.bfloat16)
-    lax.fori_loop(1, owners, tok_sent, 0)
+    everyone.wait_send()
 
 
 def embedder(channels, tokens, weight, bias, packed):
@@ -643,6 +634,7 @@
     taps = conv_weights.shape[2]
     shares = pltpu.VMEM((n, columns, parts, taps, out // columns, width // parts), jnp.bfloat16)
     cuts = CUTS if frames % CUTS == 0 else 1
+    bits = BITS if taps % BITS == 0 else 1
     tok = pltpu.VMEM((owners, SUBLANES, LANES), jnp.bfloat16)
     tokens = pl.pallas_call(
         functools.partial(encoder, n, ns, ng, nc, most, latents),
@@ -657,15 +649,12 @@
             pltpu.VMEM((1, tok_count), routes.dtype),
             field, inner,
             pltpu.VMEM((9, 3 * out, width), jnp.bfloat16),
-            shares,
+            pltpu.VMEM(shares.shape[3:], jnp.bfloat16), shares,
             pltpu.VMEM((owners * SUBLANES, tok_count), jnp.bfloat16),
             slab, slab, edge, edge, tok, tok,
-            dma((5,)), dma, dma((columns, parts)),
-            dma((n, cuts)), dma((3, cuts)), dma((n, cuts)),
-            dma((n,)), dma((n,)), dma((2, n)), dma((2, n)), dma((5,)), dma((5,)),
-            dma((n,)), dma((3,)), dma((n,)),
-            dma((n, columns)), dma((n, columns)), dma((n, columns, nc)), dma((n, columns, nc)),
-            dma((owners,)), dma((owners,)),
+            dma((5,)), dma, dma((2,)), dma((2,)), dma((3,)), dma((n, cuts)), dma((2,)), dma((2, 2)),
+            dma((5,)), dma((5,)), dma((2,)), dma((3,)), dma((n, bits)), dma((n - 1, bits)),
+            dma((3,)), dma((2,)),
         ],
         compiler_params=pltpu.CompilerParams(
             collective_id=0, has_side_effects=True, vmem_limit_bytes=GRANT

time: 41.4 us -> 40 us (0.966)
  Pallas kernels: 40.5 us -> 39.1 us
    pallas_call x1, Pallas kernels: 39.5 us -> 38.1 us  [shards(): pl.pallas_call(functools.partial(encoder, n, ns, ng, nc, most, latents),...]
where the time goes in v4:
time: 40 us; the launch traced here: 39.8 us
  Pallas kernels  39.1 us (98%)
  between operations  0.69 us (2%)
    pallas_call x1, Pallas kernels, shards(): pl.pallas_call(functools.partial(encoder, n, ns, ng, nc, most, latents),...  38.1 us
    pallas_call x1, Pallas kernels, shards(): pl.pallas_call(functools.partial(embedder, channels), grid=(embed // chun...  1.03 us

profile of v4, /device:TPU:0, one launch (start us, length us, event | category | flops | bytes accessed | tf_op | source)
XLA Modules:
  0.0 39.8 jit_solution(950829009399737314)
XLA Ops:
  0.7 0.0 copy-start
  0.7 0.0 copy-start.1
  0.7 38.1 %shard_map.91.tokens = bf16[72,128]{1,0:T(8,128)(2,1)S(1)} custom-call(bf16[4,4,16,256]{3,2,1,0:T(8,128)(2,1)} %bitcast.11, bf16[2,9,192,256]{3,2,1,0:T(8,128)(2,1)} %bitcast.9, bf16[2,27,64,256]{3,2,1,0:T(8,128)(2,1)} %bitcast.10, f32[3,256]{1,0:T(4,128)} %gains_any.1, f32[2,256]{1,0:T(2,128)} %biases_any.1, bf16[16,256]{1,0:T(8,128)(2,1)} %bitcast.12, ...), custom_call_target="tpu_custom_call" | custom-call | tf_op jit(solution)/shard_map/pallas_call | solution.py:639
  38.8 0.0 copy-done
  38.8 0.0 copy-done.1
  38.8 1.0 %shard_map.92 = bf16[72,3072]{1,0:T(8,128)(2,1)} custom-call(bf16[72,128]{1,0:T(8,128)(2,1)S(1)} %shard_map.91.tokens, bf16[64,3072]{1,0:T(8,128)(2,1)S(1)} %copy-done, f32[1,3072]{1,0:T(1,128)S(1)} %bitcast.8), custom_call_target="tpu_custom_call" | custom-call | tf_op jit(solution)/shard_map/pallas_call | solution.py:675
Async XLA Ops:
  0.7 38.1 %copy-start = (bf16[64,3072]{1,0:T(8,128)(2,1)S(1)}, bf16[64,3072]{1,0:T(8,128)(2,1)}, u32[]{:S(2)}) copy-start(bf16[64,3072]{1,0:T(8,128)(2,1)} %weight.1) | copy-start | bytes 1179652
  0.7 38.1 %copy-start.1 = (f32[3072]{0:T(1024)S(1)}, f32[3072]{0:T(1024)}, u32[]{:S(2)}) copy-start(f32[3072]{0:T(1024)} %param.17) | copy-start | bytes 36868

commit v5 on v4

--- a/solution.py
+++ b/solution.py
@@ -274,23 +274,25 @@
         return left + middle + right
 
     def one(b):
-        sums = []
-        for r in range(3):
-            total = None
-            for a in range(3):
-                block = field[pl.ds(frames * b + a, frames)]
-                term = lax.dot_general(
-                    block.reshape(cells, width), taps[3 * a + r],
-                    (((1,), (1,)), ((), ())), preferred_element_type=jnp.float32,
+        span = jnp.concatenate(
+            [field[pl.ds(frames * b + a, frames)].reshape(cells, width) for a in range(3)], axis=1
+        )
+        sums = [
+            lax.dot_general(
+                span, jnp.concatenate([taps[3 * a + r] for a in range(3)], axis=1),
+                (((1,), (1,)), ((), ())), preferred_element_type=jnp.float32,
+            ).reshape(frames, rows, cols, 3 * out)
+            for r in range(3)
+        ]
+        wide = jnp.concatenate(
+            [
+                functools.reduce(
+                    jnp.add,
+                    [sums[r][:, row : row + 1] for r in range(3) for row in [j - 2 + r] if 0 <= row < rows],
                 )
-                total = term if total is None else total + term
-            sums.append(total.reshape(frames, rows, cols, 3 * out))
-        blank = jnp.zeros((frames, 1, cols, 3 * out), jnp.float32)
-        two = jnp.concatenate([blank] * 2, axis=1)
-        wide = (
-            jnp.concatenate([sums[2], two], axis=1)
-            + jnp.concatenate([blank, sums[1], blank], axis=1)
-            + jnp.concatenate([two, sums[0]], axis=1)
+                for j in range(grid_rows)
+            ],
+            axis=1,
         ).reshape(frames * grid_rows * cols, 3 * out)
         summed = beside(wide[:, :out], wide[:, out : 2 * out], wide[:, 2 * out :])
         summed = summed.reshape(frames, grid_rows, cols, out)
@@ -389,17 +391,17 @@
     mine_load.wait()
     pl.semaphore_wait(barrier, expected)
     start = lambda copy: copy.start()
+    reach(send_blocks)
     reach(send_lines)
-    reach(send_blocks)
     weight_copy.wait()
     if relays:
         order = ((0, 1, 2, 3), (3, 2, 0, 1), (0, 3, 1, 2), (3, 2, 0, 1))
         flow = ((1, 2, 3), (0, 2, 3), (3, 1, 0), (2, 1, 0))
 
         def forward():
+            relay_block(0, 1)
             pass_on(end)
             pass_on(mate)
-            relay_block(0, 1)
             for k in range(bits):
                 line_relay(0, k).start()
                 line_relay(1, k).start()
@@ -412,10 +414,10 @@
                 pass_bit(q, k)
 
         before = (
-            ((), ((pass_on, 1), (arrived, 1)), ((arrived, 2),), ((pass_on, 2), (arrived, 3))),
+            ((), ((arrived, 1),), ((pass_on, 1), (arrived, 2)), ((pass_on, 2), (arrived, 3))),
             ((), (), ((last, 3),), ()),
             ((), (), ((last, 0),), ()),
-            (((pass_on, 2), (arrived, 2)), ((arrived, 1),), ((pass_on, 1), (arrived, 0)), ()),
+            (((arrived, 2),), ((pass_on, 2), (arrived, 1)), ((pass_on, 1), (arrived, 0)), ()),
         )
 
         def pick(table, k):

time: 40 us -> 39.2 us (0.980)
  Pallas kernels: 39.1 us -> 38.4 us
    pallas_call x1, Pallas kernels: 38.1 us -> 37.3 us  [shards(): pl.pallas_call(functools.partial(encoder, n, ns, ng, nc, most, latents),...]
where the time goes in v5:
time: 39.2 us; the launch traced here: 39.1 us
  Pallas kernels  38.4 us (98%)
  between operations  0.69 us (2%)
    pallas_call x1, Pallas kernels, shards(): pl.pallas_call(functools.partial(encoder, n, ns, ng, nc, most, latents),...  37.3 us
    pallas_call x1, Pallas kernels, shards(): pl.pallas_call(functools.partial(embedder, channels), grid=(embed // chun...  1.04 us

profile of v5, /device:TPU:0, one launch (start us, length us, event | category | flops | bytes accessed | tf_op | source)
XLA Modules:
  0.0 39.1 jit_solution(15218161967841288116)
XLA Ops:
  0.7 0.0 copy-start
  0.7 0.0 copy-start.1
  0.7 37.3 %shard_map.91.tokens = bf16[72,128]{1,0:T(8,128)(2,1)S(1)} custom-call(bf16[4,4,16,256]{3,2,1,0:T(8,128)(2,1)} %bitcast.11, bf16[2,9,192,256]{3,2,1,0:T(8,128)(2,1)} %bitcast.9, bf16[2,27,64,256]{3,2,1,0:T(8,128)(2,1)} %bitcast.10, f32[3,256]{1,0:T(4,128)} %gains_any.1, f32[2,256]{1,0:T(2,128)} %biases_any.1, bf16[16,256]{1,0:T(8,128)(2,1)} %bitcast.12, ...), custom_call_target="tpu_custom_call" | custom-call | tf_op jit(solution)/shard_map/pallas_call | solution.py:641
  38.0 0.0 copy-done
  38.0 0.0 copy-done.1
  38.0 1.0 %shard_map.92 = bf16[72,3072]{1,0:T(8,128)(2,1)} custom-call(bf16[72,128]{1,0:T(8,128)(2,1)S(1)} %shard_map.91.tokens, bf16[64,3072]{1,0:T(8,128)(2,1)S(1)} %copy-done, f32[1,3072]{1,0:T(1,128)S(1)} %bitcast.8), custom_call_target="tpu_custom_call" | custom-call | tf_op jit(solution)/shard_map/pallas_call | solution.py:677
Async XLA Ops:
  0.7 37.4 %copy-start = (bf16[64,3072]{1,0:T(8,128)(2,1)S(1)}, bf16[64,3072]{1,0:T(8,128)(2,1)}, u32[]{:S(2)}) copy-start(bf16[64,3072]{1,0:T(8,128)(2,1)} %weight.1) | copy-start | bytes 1179652
  0.7 37.4 %copy-start.1 = (f32[3072]{0:T(1024)S(1)}, f32[3072]{0:T(1024)}, u32[]{:S(2)}) copy-start(f32[3072]{0:T(1024)} %param.17) | copy-start | bytes 36868

commit v6 on v5

--- a/solution.py
+++ b/solution.py
@@ -164,11 +164,10 @@
 
     def plane_copy(q, k, d):
         piece = shares.at[q, column_of, part_of, pl.ds(bit * k, bit)]
-        peer = (column_of + d) % columns
         return pltpu.make_async_remote_copy(
             src_ref=piece, dst_ref=piece, send_sem=bulk_sem.at[0],
             recv_sem=plane_recv.at[(q - t + n) % n - 1, k],
-            device_id={"groups": peer // ns, "space": peer % ns}, device_id_type=MESH,
+            device_id={"groups": (g + d // ns) % ng, "space": (s + d % ns) % ns}, device_id_type=MESH,
         )
 
     def core_copy(q, col, k, d):
@@ -302,6 +301,14 @@
         )
         packed = fold(summed[:, 1 : rows + 1].reshape(cells, out)).astype(jnp.bfloat16)
 
+        for side in range(2):
+
+            def give(side=side):
+                edge_out[side, pl.ds(b, 1)] = fold(edges[side]).astype(jnp.bfloat16)[None]
+                edge_copy(side, t, b).start()
+
+            sided(side, give)
+
         @pl.when(b == t)
         def _():
             slab_in[pl.ds(t, 1)] = packed[None]
@@ -310,14 +317,6 @@
         def _():
             slab_out[pl.ds(b, 1)] = packed[None]
             slab_copy(t, b).start()
-
-        for side in range(2):
-
-            def give(side=side):
-                edge_out[side, pl.ds(b, 1)] = fold(edges[side]).astype(jnp.bfloat16)[None]
-                edge_copy(side, t, b).start()
-
-            sided(side, give)
 
     def halo_copies(act):
         near, far = pl.ds(frames, 2), pl.ds(0, 2)
@@ -339,9 +338,9 @@
         left, right = {"space": (s + ns - 1) % ns}, {"space": (s + 1) % ns}
         first, last = pl.ds(1, 1), pl.ds(rows, 1)
         above, below = pl.ds(0, 1), pl.ds(rows + 1, 1)
-        copy(0, more, (near, body), (far, body), up)
         copy(1, more & (s > 0), (near, first), (far, below), up | left)
         copy(2, more & (s < ns - 1), (near, last), (far, above), up | right)
+        copy(0, more, (near, body), (far, body), up)
         copy(3, s > 0, (own, first), (own, below), left)
         copy(4, s < ns - 1, (own, last), (own, above), right)
 
@@ -387,7 +386,13 @@
     same = (owner_column == owner) & (before < after)
     rank = jnp.sum(jnp.where(same, 1, 0), axis=0, keepdims=True)
     slots = lax.broadcasted_iota(jnp.int32, (owners * SUBLANES, toks), 0)
-    placing[...] = jnp.where(slots == owner * SUBLANES + rank, 1.0, 0.0).astype(jnp.bfloat16)
+    slotted = jnp.where(slots == owner * SUBLANES + rank, 1.0, 0.0).astype(jnp.bfloat16)
+    spot = lax.broadcasted_iota(jnp.int32, (toks, cells), 1)
+    patch = (spot // (2 * cols)) * (cols // 2) + spot % cols // 2
+    held = patch == lax.broadcasted_iota(jnp.int32, (toks, cells), 0)
+    placing[...] = jnp.dot(
+        slotted, jnp.where(held, 1.0, 0.0).astype(jnp.bfloat16), preferred_element_type=jnp.float32
+    ).astype(jnp.bfloat16)
     mine_load.wait()
     pl.semaphore_wait(barrier, expected)
     start = lambda copy: copy.start()
@@ -534,12 +539,6 @@
     alive = (t * frames + cell // (rows * cols) < count[0]) & (corner == 0)
     flagged = jnp.where((lane == 4 * width_latent) & alive, 1.0, 0.0)
     patches = jnp.where(lane // width_latent == corner, latent, flagged).astype(jnp.bfloat16)
-    spot = lax.broadcasted_iota(jnp.int32, (toks, cells), 1)
-    patch = (spot // (2 * cols)) * (cols // 2) + spot % cols // 2
-    mine = patch == lax.broadcasted_iota(jnp.int32, (toks, cells), 0)
-    patches = jnp.dot(
-        jnp.where(mine, 1.0, 0.0).astype(jnp.bfloat16), patches, preferred_element_type=jnp.float32
-    ).astype(jnp.bfloat16)
     outgoing = jnp.dot(
         placing[...], patches, preferred_element_type=jnp.float32
     ).astype(jnp.bfloat16)
@@ -652,7 +651,7 @@
             field, inner,
             pltpu.VMEM((9, 3 * out, width), jnp.bfloat16),
             pltpu.VMEM(shares.shape[3:], jnp.bfloat16), shares,
-            pltpu.VMEM((owners * SUBLANES, tok_count), jnp.bfloat16),
+            pltpu.VMEM((owners * SUBLANES, cells), jnp.bfloat16),
             slab, slab, edge, edge, tok, tok,
             dma((5,)), dma, dma((2,)), dma((2,)), dma((3,)), dma((n, cuts)), dma((2,)), dma((2, 2)),
             dma((5,)), dma((5,)), dma((2,)), dma((3,)), dma((n, bits)), dma((n - 1, bits)),

time: 39.2 us -> 39.2 us (level)
  no operation moved by 1% of the time
where the time goes in v6:
time: 39.2 us; the launch traced here: 39 us
  Pallas kernels  38.3 us (98%)
  between operations  0.69 us (2%)
    pallas_call x1, Pallas kernels, shards(): pl.pallas_call(functools.partial(encoder, n, ns, ng, nc, most, latents),...  37.3 us
    pallas_call x1, Pallas kernels, shards(): pl.pallas_call(functools.partial(embedder, channels), grid=(embed // chun...  1.03 us

profile of v6, /device:TPU:0, one launch (start us, length us, event | category | flops | bytes accessed | tf_op | source)
XLA Modules:
  0.0 39.0 jit_solution(300379514534723479)
XLA Ops:
  0.7 0.0 copy-start
  0.7 0.0 copy-start.1
  0.7 37.3 %shard_map.91.tokens = bf16[72,128]{1,0:T(8,128)(2,1)S(1)} custom-call(bf16[4,4,16,256]{3,2,1,0:T(8,128)(2,1)} %bitcast.11, bf16[2,9,192,256]{3,2,1,0:T(8,128)(2,1)} %bitcast.9, bf16[2,27,64,256]{3,2,1,0:T(8,128)(2,1)} %bitcast.10, f32[3,256]{1,0:T(4,128)} %gains_any.1, f32[2,256]{1,0:T(2,128)} %biases_any.1, bf16[16,256]{1,0:T(8,128)(2,1)} %bitcast.12, ...), custom_call_target="tpu_custom_call" | custom-call | tf_op jit(solution)/shard_map/pallas_call | solution.py:640
  37.9 0.0 copy-done
  38.0 0.0 copy-done.1
  38.0 1.0 %shard_map.92 = bf16[72,3072]{1,0:T(8,128)(2,1)} custom-call(bf16[72,128]{1,0:T(8,128)(2,1)S(1)} %shard_map.91.tokens, bf16[64,3072]{1,0:T(8,128)(2,1)S(1)} %copy-done, f32[1,3072]{1,0:T(1,128)S(1)} %bitcast.8), custom_call_target="tpu_custom_call" | custom-call | tf_op jit(solution)/shard_map/pallas_call | solution.py:676
Async XLA Ops:
  0.7 37.3 %copy-start = (bf16[64,3072]{1,0:T(8,128)(2,1)S(1)}, bf16[64,3072]{1,0:T(8,128)(2,1)}, u32[]{:S(2)}) copy-start(bf16[64,3072]{1,0:T(8,128)(2,1)} %weight.1) | copy-start | bytes 1179652
  0.7 37.3 %copy-start.1 = (f32[3072]{0:T(1024)S(1)}, f32[3072]{0:T(1024)}, u32[]{:S(2)}) copy-start(f32[3072]{0:T(1024)} %param.17) | copy-start | bytes 36868

commit v7 on v6

--- a/solution.py
+++ b/solution.py
@@ -10,7 +10,7 @@
 MESH = pl.DeviceIdType.MESH
 LANES = 128
 SUBLANES = 16
-CUTS = 4
+CUTS = 2
 BITS = 3
 GRANT = 28 << 20
 
@@ -27,7 +27,7 @@
     tokens_out,
     feat, gains, biases, latent_rows, owner_of, field, inner, taps, mine, shares, placing, slab_out, slab_in, edge_out, edge_in, tok_out, tok_in,
     load_sem, raw_sem, share_sem, block_send, relay_send, block_recv, slab_sem, edge_sem,
-    halo_send, halo_recv, line_send, line_relay_send, line_recv, plane_recv, bulk_sem, tok_sem,
+    halo_recv, line_send, line_relay_send, line_recv, plane_recv, bulk_sem, tok_sem,
 ):
     t = lax.axis_index("tm")
     s = lax.axis_index("space")
@@ -329,7 +329,7 @@
                 lambda: act(
                     pltpu.make_async_remote_copy(
                         src_ref=inner.at[source], dst_ref=inner.at[target],
-                        send_sem=halo_send.at[i], recv_sem=halo_recv.at[i],
+                        send_sem=load_sem.at[i], recv_sem=halo_recv.at[i],
                         device_id=device, device_id_type=MESH,
                     )
                 )
@@ -349,7 +349,7 @@
             def act():
                 span = inner.at[target]
                 pltpu.make_async_remote_copy(
-                    src_ref=span, dst_ref=span, send_sem=halo_send.at[i],
+                    src_ref=span, dst_ref=span, send_sem=load_sem.at[i],
                     recv_sem=halo_recv.at[i], device_id={"tm": t}, device_id_type=MESH,
                 ).wait_recv()
 
@@ -420,7 +420,7 @@
 
         before = (
             ((), ((arrived, 1),), ((pass_on, 1), (arrived, 2)), ((pass_on, 2), (arrived, 3))),
-            ((), (), ((last, 3),), ()),
+            ((), ((last, 3),), (), ()),
             ((), (), ((last, 0),), ()),
             (((arrived, 2),), ((pass_on, 2), (arrived, 1)), ((pass_on, 1), (arrived, 0)), ()),
         )
@@ -654,7 +654,7 @@
             pltpu.VMEM((owners * SUBLANES, cells), jnp.bfloat16),
             slab, slab, edge, edge, tok, tok,
             dma((5,)), dma, dma((2,)), dma((2,)), dma((3,)), dma((n, cuts)), dma((2,)), dma((2, 2)),
-            dma((5,)), dma((5,)), dma((2,)), dma((3,)), dma((n, bits)), dma((n - 1, bits)),
+            dma((5,)), dma((2,)), dma((3,)), dma((n, bits)), dma((n - 1, bits)),
             dma((3,)), dma((2,)),
         ],
         compiler_params=pltpu.CompilerParams(

time: 39.2 us -> 39 us (level)
  no operation moved by 1% of the time
where the time goes in v7:
time: 39 us; the launch traced here: 38.9 us
  Pallas kernels  38.2 us (98%)
  between operations  0.69 us (2%)
    pallas_call x1, Pallas kernels, shards(): pl.pallas_call(functools.partial(encoder, n, ns, ng, nc, most, latents),...  37.1 us
    pallas_call x1, Pallas kernels, shards(): pl.pallas_call(functools.partial(embedder, channels), grid=(embed // chun...  1.03 us

profile of v7, /device:TPU:0, one launch (start us, length us, event | category | flops | bytes accessed | tf_op | source)
XLA Modules:
  0.0 38.9 jit_solution(8711674800336616832)
XLA Ops:
  0.7 0.0 copy-start
  0.7 0.0 copy-start.1
  0.7 37.1 %shard_map.91.tokens = bf16[72,128]{1,0:T(8,128)(2,1)S(1)} custom-call(bf16[4,4,16,256]{3,2,1,0:T(8,128)(2,1)} %bitcast.11, bf16[2,9,192,256]{3,2,1,0:T(8,128)(2,1)} %bitcast.9, bf16[2,27,64,256]{3,2,1,0:T(8,128)(2,1)} %bitcast.10, f32[3,256]{1,0:T(4,128)} %gains_any.1, f32[2,256]{1,0:T(2,128)} %biases_any.1, bf16[16,256]{1,0:T(8,128)(2,1)} %bitcast.12, ...), custom_call_target="tpu_custom_call" | custom-call | tf_op jit(solution)/shard_map/pallas_call | solution.py:640
  37.8 0.0 copy-done
  37.8 0.0 copy-done.1
  37.8 1.0 %shard_map.92 = bf16[72,3072]{1,0:T(8,128)(2,1)} custom-call(bf16[72,128]{1,0:T(8,128)(2,1)S(1)} %shard_map.91.tokens, bf16[64,3072]{1,0:T(8,128)(2,1)S(1)} %copy-done, f32[1,3072]{1,0:T(1,128)S(1)} %bitcast.8), custom_call_target="tpu_custom_call" | custom-call | tf_op jit(solution)/shard_map/pallas_call | solution.py:676
Async XLA Ops:
  0.7 37.2 %copy-start = (bf16[64,3072]{1,0:T(8,128)(2,1)S(1)}, bf16[64,3072]{1,0:T(8,128)(2,1)}, u32[]{:S(2)}) copy-start(bf16[64,3072]{1,0:T(8,128)(2,1)} %weight.1) | copy-start | bytes 1179652
  0.7 37.2 %copy-start.1 = (f32[3072]{0:T(1024)S(1)}, f32[3072]{0:T(1024)}, u32[]{:S(2)}) copy-start(f32[3072]{0:T(1024)} %param.17) | copy-start | bytes 36868

commit v8 on v7

--- a/solution.py
+++ b/solution.py
@@ -400,7 +400,7 @@
     reach(send_lines)
     weight_copy.wait()
     if relays:
-        order = ((0, 1, 2, 3), (3, 2, 0, 1), (0, 3, 1, 2), (3, 2, 0, 1))
+        order = ((0, 1, 2, 3), (3, 2, 0, 1), (0, 1, 3, 2), (3, 2, 0, 1))
         flow = ((1, 2, 3), (0, 2, 3), (3, 1, 0), (2, 1, 0))
 
         def forward():

time: 39 us -> 39 us (level)
  no operation moved by 1% of the time
where the time goes in v8:
time: 39 us; the launch traced here: 38.9 us
  Pallas kernels  38.2 us (98%)
  between operations  0.69 us (2%)
    pallas_call x1, Pallas kernels, shards(): pl.pallas_call(functools.partial(encoder, n, ns, ng, nc, most, latents),...  37.1 us
    pallas_call x1, Pallas kernels, shards(): pl.pallas_call(functools.partial(embedder, channels), grid=(embed // chun...  1.03 us

profile of v8, /device:TPU:0, one launch (start us, length us, event | category | flops | bytes accessed | tf_op | source)
XLA Modules:
  0.0 38.9 jit_solution(6249831451391100113)
XLA Ops:
  0.7 0.0 copy-start
  0.7 0.0 copy-start.1
  0.7 37.1 %shard_map.91.tokens = bf16[72,128]{1,0:T(8,128)(2,1)S(1)} custom-call(bf16[4,4,16,256]{3,2,1,0:T(8,128)(2,1)} %bitcast.11, bf16[2,9,192,256]{3,2,1,0:T(8,128)(2,1)} %bitcast.9, bf16[2,27,64,256]{3,2,1,0:T(8,128)(2,1)} %bitcast.10, f32[3,256]{1,0:T(4,128)} %gains_any.1, f32[2,256]{1,0:T(2,128)} %biases_any.1, bf16[16,256]{1,0:T(8,128)(2,1)} %bitcast.12, ...), custom_call_target="tpu_custom_call" | custom-call | tf_op jit(solution)/shard_map/pallas_call | solution.py:640
  37.8 0.0 copy-done
  37.8 0.0 copy-done.1
  37.8 1.0 %shard_map.92 = bf16[72,3072]{1,0:T(8,128)(2,1)} custom-call(bf16[72,128]{1,0:T(8,128)(2,1)S(1)} %shard_map.91.tokens, bf16[64,3072]{1,0:T(8,128)(2,1)S(1)} %copy-done, f32[1,3072]{1,0:T(1,128)S(1)} %bitcast.8), custom_call_target="tpu_custom_call" | custom-call | tf_op jit(solution)/shard_map/pallas_call | solution.py:676
Async XLA Ops:
  0.7 37.2 %copy-start = (bf16[64,3072]{1,0:T(8,128)(2,1)S(1)}, bf16[64,3072]{1,0:T(8,128)(2,1)}, u32[]{:S(2)}) copy-start(bf16[64,3072]{1,0:T(8,128)(2,1)} %weight.1) | copy-start | bytes 1179652
  0.7 37.2 %copy-start.1 = (f32[3072]{0:T(1024)S(1)}, f32[3072]{0:T(1024)}, u32[]{:S(2)}) copy-start(f32[3072]{0:T(1024)} %param.17) | copy-start | bytes 36868
